TPU v7x, 32 devices: a whole 2x2x4 slice. The times are simulated.
32 devices in a mesh: left: 8 (over y, x, core), right: 4 (over z).
Axes of the slice: x: 2, y: 2, z: 4, core: 2. Of those that a mesh axis runs over, the one named last changes fastest.
Arguments:
- left_freq: float32 [16384], P('left'), as said below
- right_freq: float32 [16384], P('right'), as said below
- left_dirs: float32 [16, 16384], P(None, 'left'), may hold values from -6 to 6
- left_data: float32 [16, 16384], P(None, 'left'), may hold values from -6 to 6
- right_dirs: float32 [16, 16384], P(None, 'right'), may hold values from -6 to 6
- right_data: float32 [16, 16384], P(None, 'right'), may hold values from -6 to 6
- col_sketch: bfloat16 [16384, 256], P('right'), may hold values from -0.047265625 to 0.047265625
- row_sketch: bfloat16 [16384, 256], P('left'), may hold values from -0.047265625 to 0.047265625
Outputs:
- row_scaled: float32 [16384, 256], P(('left', 'right'))
- col_scaled: float32 [16384, 256], P('right')
- lower_reduced: float32 [256, 256], replicated
- shifted_reduced: float32 [256, 256], replicated
Inputs may be any that keep to these rules, and one draw needn't show every extreme that they name: left_freq[i] = 1 + (k + e) / 16384 with k distinct whole numbers of 0 to 16383 and |e| at most 0.2. right_freq[j] = 1 + (k + 0.5 + e) / 16384 with k distinct whole numbers of 0 to 16383 and |e| at most 0.2; left and right frequencies share the spacing 1 / 16384, so every left and right frequency differ by 0.1 / 16384 or more.
All inputs are finite; a program needn't handle non-finite values.
Results may differ from a plain program's by a relative error of at most 0.0089.
Values sent between devices are 32-bit elements; how exact they have to be, the bound alone decides.
A program may use at most 256 MiB of HBM per device.

v0:
```python
import math

import jax
import jax.numpy as jnp
from jax import lax
from jax.sharding import PartitionSpec as P

precise = lax.Precision.HIGHEST


def build_tiles(freq_rows, dirs_rows, data_rows, right_freq, right_dirs, right_data, total_rows):
    direct = lax.dot_general(
        data_rows,
        right_dirs,
        (((0,), (0,)), ((), ())),
        precision=precise,
        preferred_element_type=jnp.float32,
    )
    crossed = lax.dot_general(
        dirs_rows,
        right_data,
        (((0,), (0,)), ((), ())),
        precision=precise,
        preferred_element_type=jnp.float32,
    )
    spacing_gap = total_rows * (freq_rows[:, None] - right_freq[None, :])
    lower_tile = ((direct - crossed) / spacing_gap).astype(jnp.bfloat16)
    shift_tile = (
        (freq_rows[:, None] * direct - right_freq[None, :] * crossed) / spacing_gap
    ).astype(jnp.bfloat16)
    return (lower_tile, shift_tile)


def gram_of(basis):
    return lax.dot_general(
        basis,
        basis,
        (((0,), (0,)), ((), ())),
        precision=precise,
        preferred_element_type=jnp.float32,
    )


def apply_factor(basis, gram_sum, shifted_flag):
    width = gram_sum.shape[0]
    identity = jnp.eye(width, dtype=jnp.float32)
    if shifted_flag:
        gram_sum = gram_sum + 1e-05 * jnp.trace(gram_sum) / width * identity
    factor = jnp.linalg.cholesky(gram_sum)
    inverse = jax.scipy.linalg.solve_triangular(factor, identity, lower=True)
    return lax.dot_general(
        basis,
        inverse,
        (((1,), (1,)), ((), ())),
        precision=precise,
        preferred_element_type=jnp.float32,
    )


def body(
    left_freq, right_freq, left_dirs, left_data, right_dirs, right_data, col_sketch, row_sketch
):
    row_count = left_freq.shape[0]
    col_count = right_freq.shape[0]
    total_rows = row_count * lax.axis_size("left")
    total_cols = col_count * lax.axis_size("right")
    lower_tile, shift_tile = build_tiles(
        left_freq, left_dirs, left_data, right_freq, right_dirs, right_data, total_rows
    )
    row_image = lax.psum(
        jnp.dot(lower_tile, col_sketch, preferred_element_type=jnp.float32), "right"
    )
    col_image = lax.psum(
        lax.dot_general(
            lower_tile, row_sketch, (((0,), (0,)), ((), ())), preferred_element_type=jnp.float32
        ),
        "left",
    )
    row_full, col_full = (row_image, col_image)
    for sweep_index in range(2):
        gram_rows = lax.psum(gram_of(row_full), "left")
        gram_cols = lax.psum(gram_of(col_full), "right")
        row_full = apply_factor(row_full, gram_rows, sweep_index == 0)
        col_full = apply_factor(col_full, gram_cols, sweep_index == 0)
    share_rows = row_count // lax.axis_size("right")
    row_part = lax.dynamic_slice_in_dim(
        row_full, lax.axis_index("right") * share_rows, share_rows, 0
    )
    col_round = col_full.astype(jnp.bfloat16)
    lower_applied = jnp.dot(lower_tile, col_round, preferred_element_type=jnp.float32)
    shift_applied = jnp.dot(shift_tile, col_round, preferred_element_type=jnp.float32)
    lower_part = lax.dot_general(
        row_full,
        lower_applied,
        (((0,), (0,)), ((), ())),
        precision=precise,
        preferred_element_type=jnp.float32,
    )
    shift_part = lax.dot_general(
        row_full,
        shift_applied,
        (((0,), (0,)), ((), ())),
        precision=precise,
        preferred_element_type=jnp.float32,
    )
    lower_reduced, shifted_reduced = lax.psum((lower_part, shift_part), ("left", "right"))
    return (
        row_part * math.sqrt(total_rows),
        col_full * math.sqrt(total_cols),
        lower_reduced,
        shifted_reduced,
    )


def solution(mesh):
    in_specs = (
        P("left"),
        P("right"),
        P(None, "left"),
        P(None, "left"),
        P(None, "right"),
        P(None, "right"),
        P("right", None),
        P("left", None),
    )
    out_specs = (P(("left", "right"), None), P("right", None), P(), P())
    return jax.shard_map(body, mesh=mesh, in_specs=in_specs, out_specs=out_specs, check_vma=False)
```

profile of v0, /device:TPU:0, one launch (start us, length us, event | category | flops | bytes accessed | tf_op | source)
XLA Modules:
  0.0 872.2 jit_solution(7962259193701451676)
XLA Ops:
  7.3 31.2 %fusion.62 = f32[2048,4096]{1,0:T(8,128)} fusion(f32[16,2048]{1,0:T(8,128)} %param.13, f32[16,4096]{1,0:T(8,128)} %param.16), kind=kOutput, calls=%fused_computation.136 | convolution fusion | flops 1610612736 | bytes 33947648 | tf_op jit(solution)/shard_map/dot_general | solution.py:19
  38.5 39.8 %divide_convert_fusion.1 = (bf16[2048,4096]{1,0:T(8,128)(2,1)}, f32[2048,4096]{1,0:T(8,128)}) fusion(f32[2048,4096]{1,0:T(8,128)} %fusion.62, f32[4096]{0:T(1024)S(1)} %copy-done.8, f32[2048]{0:T(1024)S(1)} %copy-done.9, f32[16,2048]{1,0:T(8,128)S(1)} %copy-done.7, f32[16,4096]{1,0:T(8,128)S(1)} %copy-done.6), kind=kOutput, calls=%fused_computation.9 | convolution fusion | flops 1652555776 | bytes 84303872 | tf_op jit(solution)/shard_map/dot_general | solution.py:12
  78.3 9.6 %fusion.63 = f32[2048,256]{1,0:T(8,128)} fusion(bf16[2048,4096]{1,0:T(8,128)(2,1)} %get-tuple-element.96, bf16[4096,256]{1,0:T(8,128)(2,1)S(1)} %copy-done), kind=kOutput, calls=%fused_computation.137 | convolution fusion | flops 4294967296 | bytes 20971520 | tf_op jit(solution)/shard_map/dot_general | solution.py:71
  87.9 10.6 %fusion.66 = f32[4096,256]{1,0:T(8,128)} fusion(bf16[2048,4096]{1,0:T(8,128)(2,1)} %get-tuple-element.96, bf16[2048,256]{1,0:T(8,128)(2,1)S(1)} %copy-done.5), kind=kOutput, calls=%fused_computation.140 | convolution fusion | flops 4294967296 | bytes 22020096 | tf_op jit(solution)/shard_map/dot_general | solution.py:74
  98.5 78.8 %all-reduce.10.cloned.1.call-done = f32[2048,256]{1,0:T(8,128)} async-done(((f32[2048,256]{1,0:T(8,128)}), f32[2048,256]{1,0:T(8,128)}) %all-reduce.10.cloned.1.call-update) | async-done | bytes 2097168 | tf_op jit(solution)/shard_map/psum | solution.py:70
  184.2 52.1 %all-reduce.12.cloned.1.call-done = f32[256,256]{0,1:T(8,128)} async-done(((f32[256,256]{0,1:T(8,128)}), f32[256,256]{0,1:T(8,128)}) %all-reduce.12.cloned.1.call-update) | async-done | bytes 262160 | tf_op jit(solution)/shard_map/psum | solution.py:81
  240.7 11.7 %cholesky.214 = f32[128,128]{1,0:T(8,128)S(1)} custom-call(f32[128,128]{1,0:T(8,128)S(1)} %cholesky.346), custom_call_target="Cholesky" | custom-call | tf_op jit(solution)/shard_map/jit(cholesky)/cholesky | solution.py:49
  252.4 9.8 %custom-call.17 = f32[1,128,128]{1,2,0:T(8,128)S(1)} custom-call(f32[1,128,128]{2,1,0:T(8,128)S(1)} %get-tuple-element.95), custom_call_target="InvertDiagBlocksLowerTriangular" | custom-call | tf_op jit(solution)/shard_map/jit(cholesky)/cholesky | solution.py:49
  262.7 11.7 %cholesky.231 = f32[128,128]{1,0:T(8,128)S(1)} custom-call(f32[128,128]{1,0:T(8,128)S(1)} %convolution_subtract_fusion.7), custom_call_target="Cholesky" | custom-call | tf_op jit(solution)/shard_map/jit(cholesky)/cholesky | solution.py:49
  280.7 19.7 %custom-call.18 = f32[2,128,128]{1,2,0:T(8,128)S(1)} custom-call(f32[2,128,128]{2,1,0:T(8,128)S(1)} %get-tuple-element.32), custom_call_target="InvertDiagBlocksLowerTriangular" | custom-call | tf_op jit(solution)/shard_map/jit(_solve_triangular)/triangular_solve | solution.py:50
  309.3 83.4 %all-reduce.20.cloned.1.call-done = (f32[256,256]{0,1:T(8,128)}, f32[4096,256]{1,0:T(8,128)}) async-done(((f32[256,256]{0,1:T(8,128)}, f32[4096,256]{1,0:T(8,128)}), (f32[256,256]{0,1:T(8,128)}, f32[4096,256]{1,0:T(8,128)})) %all-reduce.20.cloned.1.call-update) | async-done | bytes 4456464 | tf_op jit(solution)/shard_map/psum | solution.py:81
  394.8 11.7 %cholesky.248 = f32[128,128]{1,0:T(8,128)S(1)} custom-call(f32[128,128]{1,0:T(8,128)S(1)} %cholesky.349), custom_call_target="Cholesky" | custom-call | tf_op jit(solution)/shard_map/jit(cholesky)/cholesky | solution.py:49
  407.2 9.8 %custom-call.19 = f32[1,128,128]{1,2,0:T(8,128)S(1)} custom-call(f32[1,128,128]{2,1,0:T(8,128)S(1)} %get-tuple-element.91), custom_call_target="InvertDiagBlocksLowerTriangular" | custom-call | tf_op jit(solution)/shard_map/jit(cholesky)/cholesky | solution.py:49
  417.5 11.7 %cholesky.265 = f32[128,128]{1,0:T(8,128)S(1)} custom-call(f32[128,128]{1,0:T(8,128)S(1)} %convolution_subtract_fusion.6), custom_call_target="Cholesky" | custom-call | tf_op jit(solution)/shard_map/jit(cholesky)/cholesky | solution.py:49
  435.7 19.7 %custom-call.20 = f32[2,128,128]{1,2,0:T(8,128)S(1)} custom-call(f32[2,128,128]{2,1,0:T(8,128)S(1)} %get-tuple-element.33), custom_call_target="InvertDiagBlocksLowerTriangular" | custom-call | tf_op jit(solution)/shard_map/jit(_solve_triangular)/triangular_solve | solution.py:50
  455.7 10.9 %fusion.67 = f32[256,256]{0,1:T(8,128)} fusion(f32[4096,256]{1,0:T(8,128)} %get-tuple-element.71), kind=kOutput, calls=%fused_computation.141 | convolution fusion | flops 3221225472 | bytes 4456448 | tf_op jit(solution)/shard_map/dot_general | solution.py:35
  467.6 34.6 %all-reduce.14.cloned.1.call-done = f32[256,256]{0,1:T(8,128)} async-done(((f32[256,256]{0,1:T(8,128)}), f32[256,256]{0,1:T(8,128)}) %all-reduce.14.cloned.1.call-update) | async-done | bytes 262160 | tf_op jit(solution)/shard_map/psum | solution.py:82
  506.6 11.7 %cholesky.282 = f32[128,128]{1,0:T(8,128)S(1)} custom-call(f32[128,128]{1,0:T(8,128)S(1)} %cholesky.352), custom_call_target="Cholesky" | custom-call | tf_op jit(solution)/shard_map/jit(cholesky)/cholesky | solution.py:49
  519.0 9.8 %custom-call.21 = f32[1,128,128]{1,2,0:T(8,128)S(1)} custom-call(f32[1,128,128]{2,1,0:T(8,128)S(1)} %get-tuple-element.87), custom_call_target="InvertDiagBlocksLowerTriangular" | custom-call | tf_op jit(solution)/shard_map/jit(cholesky)/cholesky | solution.py:49
  529.3 11.7 %cholesky.299 = f32[128,128]{1,0:T(8,128)S(1)} custom-call(f32[128,128]{1,0:T(8,128)S(1)} %convolution_subtract_fusion.5), custom_call_target="Cholesky" | custom-call | tf_op jit(solution)/shard_map/jit(cholesky)/cholesky | solution.py:49
  547.2 19.7 %custom-call.22 = f32[2,128,128]{1,2,0:T(8,128)S(1)} custom-call(f32[2,128,128]{2,1,0:T(8,128)S(1)} %get-tuple-element.34), custom_call_target="InvertDiagBlocksLowerTriangular" | custom-call | tf_op jit(solution)/shard_map/jit(_solve_triangular)/triangular_solve | solution.py:50
  575.2 7.4 fusion.68
  586.3 31.6 %all-reduce.16.cloned.1.call-done = f32[256,256]{0,1:T(8,128)} async-done(((f32[256,256]{0,1:T(8,128)}), f32[256,256]{0,1:T(8,128)}) %all-reduce.16.cloned.1.call-update) | async-done | bytes 262160 | tf_op jit(solution)/shard_map/psum | solution.py:82
  620.0 11.7 %cholesky.316 = f32[128,128]{1,0:T(8,128)S(1)} custom-call(f32[128,128]{1,0:T(8,128)S(1)} %cholesky.355), custom_call_target="Cholesky" | custom-call | tf_op jit(solution)/shard_map/jit(cholesky)/cholesky | solution.py:49
  632.4 9.8 %custom-call.23 = f32[1,128,128]{1,2,0:T(8,128)S(1)} custom-call(f32[1,128,128]{2,1,0:T(8,128)S(1)} %get-tuple-element.83), custom_call_target="InvertDiagBlocksLowerTriangular" | custom-call | tf_op jit(solution)/shard_map/jit(cholesky)/cholesky | solution.py:49
  642.7 11.9 %cholesky.333 = f32[128,128]{1,0:T(8,128)S(1)} custom-call(f32[128,128]{1,0:T(8,128)S(1)} %convolution_subtract_fusion.4), custom_call_target="Cholesky" | custom-call | tf_op jit(solution)/shard_map/jit(cholesky)/cholesky | solution.py:49
  660.6 19.7 %custom-call.24 = f32[2,128,128]{1,2,0:T(8,128)S(1)} custom-call(f32[2,128,128]{2,1,0:T(8,128)S(1)} %get-tuple-element.35), custom_call_target="InvertDiagBlocksLowerTriangular" | custom-call | tf_op jit(solution)/shard_map/jit(_solve_triangular)/triangular_solve | solution.py:50
  681.3 7.7 broadcast_multiply_fusion
  689.0 9.5 %fusion.2 = f32[2048,256]{1,0:T(8,128)} fusion(bf16[2048,4096]{1,0:T(8,128)(2,1)} %get-tuple-element.96, bf16[4096,256]{1,0:T(8,128)(2,1)S(1)} %get-tuple-element.107), kind=kOutput, calls=%fused_computation.22 | convolution fusion | flops 4294967296 | bytes 20971520 | tf_op jit(solution)/shard_map/dot_general | solution.py:90
  698.4 24.4 %fusion = f32[2048,256]{1,0:T(8,128)} fusion(f32[2048,4096]{1,0:T(8,128)} %fusion.62, f32[2048,4096]{1,0:T(8,128)} %get-tuple-element.97, f32[4096]{0:T(1024)S(1)} %copy-done.8, f32[2048]{0:T(1024)S(1)} %copy-done.9, bf16[4096,256]{1,0:T(8,128)(2,1)S(1)} %get-tuple-element.107), kind=kOutput, calls=%fused_computation.11 | convolution fusion | flops 4353687552 | bytes 71327744 | tf_op jit(solution)/shard_map/dot_general | solution.py:91
  722.9 6.5 fusion.69
  735.7 126.1 %all-reduce.18.cloned.1.call-done = (f32[256,256]{1,0:T(8,128)}, f32[256,256]{1,0:T(8,128)}) async-done(((f32[256,256]{1,0:T(8,128)}, f32[256,256]{1,0:T(8,128)}), (f32[256,256]{1,0:T(8,128)}, f32[256,256]{1,0:T(8,128)})) %all-reduce.18.cloned.1.call-update) | async-done | bytes 524304 | tf_op jit(solution)/shard_map/psum | solution.py:106
  (135 shorter events, 90.7 us)
Async XLA Ops:
  7.2 71.1 %copy-start = (bf16[4096,256]{1,0:T(8,128)(2,1)S(1)}, bf16[4096,256]{1,0:T(8,128)(2,1)}, u32[]{:S(2)}) copy-start(bf16[4096,256]{1,0:T(8,128)(2,1)} %param.17) | copy-start | bytes 6291460
  7.2 31.3 %copy-start.8 = (f32[4096]{0:T(1024)S(1)}, f32[4096]{0:T(1024)}, u32[]{:S(2)}) copy-start(f32[4096]{0:T(1024)} %param.12) | copy-start | bytes 49156
  7.2 31.3 %copy-start.9 = (f32[2048]{0:T(1024)S(1)}, f32[2048]{0:T(1024)}, u32[]{:S(2)}) copy-start(f32[2048]{0:T(1024)} %param.11) | copy-start | bytes 24580
  7.2 31.3 %copy-start.6 = (f32[16,4096]{1,0:T(8,128)S(1)}, f32[16,4096]{1,0:T(8,128)}, u32[]{:S(2)}) copy-start(f32[16,4096]{1,0:T(8,128)} %param.15) | copy-start | bytes 786436
  7.2 31.3 %copy-start.7 = (f32[16,2048]{1,0:T(8,128)S(1)}, f32[16,2048]{1,0:T(8,128)}, u32[]{:S(2)}) copy-start(f32[16,2048]{1,0:T(8,128)} %param.14) | copy-start | bytes 393220
  7.2 170.0 %all-reduce.10.cloned.1.call-start = ((), (), s32[]{:S(2)}) async-start(), calls=%async_computation | async-start | bytes 4194304 | tf_op jit(solution)/shard_map/psum | solution.py:70
  78.3 9.6 %copy-start.5 = (bf16[2048,256]{1,0:T(8,128)(2,1)S(1)}, bf16[2048,256]{1,0:T(8,128)(2,1)}, u32[]{:S(2)}) copy-start(bf16[2048,256]{1,0:T(8,128)(2,1)} %param.18) | copy-start | bytes 3145732
  87.9 148.4 %all-reduce.12.cloned.1.call-start = ((), (), s32[]{:S(2)}) async-start(), calls=%async_computation.1 | async-start | bytes 524288 | tf_op jit(solution)/shard_map/psum | solution.py:81
  183.7 209.1 %all-reduce.20.cloned.1.call-start = ((), (), s32[]{:S(2)}) async-start(), calls=%async_computation.5 | async-start | bytes 8912896 | tf_op jit(solution)/shard_map/psum | solution.py:81
  309.1 193.1 %all-reduce.14.cloned.1.call-start = ((), (), s32[]{:S(2)}) async-start(), calls=%async_computation.2 | async-start | bytes 524288 | tf_op jit(solution)/shard_map/psum | solution.py:82
  466.6 151.3 %all-reduce.16.cloned.1.call-start = ((), (), s32[]{:S(2)}) async-start(), calls=%async_computation.3 | async-start | bytes 524288 | tf_op jit(solution)/shard_map/psum | solution.py:82
  573.3 2.0 copy-start.2
  582.7 279.1 %all-reduce.18.cloned.1.call-start = ((), (), s32[]{:S(2)}) async-start(), calls=%async_computation.4 | async-start | bytes 1048576 | tf_op jit(solution)/shard_map/psum | solution.py:106
  722.9 6.6 copy-start.3
  722.9 6.6 copy-start.4
  722.9 142.2 %copy-start.1 = (bf16[4096,256]{1,0:T(8,128)(2,1)S(1)}, bf16[4096,256]{1,0:T(8,128)(2,1)}, u32[]{:S(2)}) copy-start(bf16[4096,256]{1,0:T(8,128)(2,1)} %param.17) | copy-start | bytes 6291460
Sparse Core Ops, SparseCore 0:
  88.0 89.2 all-reduce.9
  183.8 52.4 all-reduce.11
  309.2 83.4 all-reduce.19
  466.7 35.4 all-reduce.13
  582.8 35.0 all-reduce.15
  733.9 127.8 all-reduce.17
where the time goes:
time: 878 us; the launch traced here: 872 us
  waiting for transfers between devices  407 us (46%)
  other arithmetic  228 us (26%)
  matrix products  190 us (22%)
  local copies, waits for them, and re-layouts  23.8 us (3%)
  between operations  21.4 us (2%)
    another operation x27, other arithmetic, apply_factor(): factor = jnp.linalg.cholesky(gram_sum)  138 us
    psum x2, waiting for transfers between devices, body(): gram_rows = lax.psum(gram_of(row_full), 'left')  135 us
    psum x1, waiting for transfers between devices, body(): lax.psum((lower_part, shift_part), ('left', 'right'))  126 us
    another operation x9, other arithmetic, apply_factor(): inverse = jax.scipy.linalg.solve_triangular(factor, identity, lower=True)  78.8 us
    psum x1, waiting for transfers between devices, body(): lax.psum(jnp.dot(lower_tile, col_sketch, preferred_element_type=jnp.float...  78.8 us
    psum x2, waiting for transfers between devices, body(): gram_cols = lax.psum(gram_of(col_full), 'right')  66.2 us
    dot_general x1, matrix products, build_tiles(): lax.dot_general(data_rows, right_dirs, (((0,), (0,)), ((), ())), precisio...  39.8 us
    dot_general x1, matrix products, build_tiles(): lax.dot_general(dirs_rows, right_data, (((0,), (0,)), ((), ())), precisio...  31.2 us
  transfers between devices with their start and end apart: 6, of which 6 were waited for; matrix products, arithmetic and copies ran while one was open for 2% of the time, Pallas kernels for 0%

commit v1 on v0

v1 whole, which is shorter than its diff:
```python
import functools
import math

import jax
import jax.numpy as jnp
from jax import lax
from jax.experimental import pallas as pl
from jax.experimental.pallas import tpu as pltpu
from jax.sharding import PartitionSpec as P

precise = lax.Precision.HIGHEST
F32 = jnp.float32
BF16 = jnp.bfloat16
LEFT_PARTS = (0, 0, 1, 0, 1, 2)
RIGHT_PARTS = (0, 1, 0, 2, 1, 0)


def tdot(a, b, precision=None):
    return lax.dot_general(
        a, b, (((0,), (0,)), ((), ())), precision=precision, preferred_element_type=F32
    )


def split3(x):
    one = x.astype(BF16).astype(F32)
    rest = x - one
    two = rest.astype(BF16).astype(F32)
    return (one, two, (rest - two).astype(BF16).astype(F32))


def stack_parts(first, second, order):
    a, b = split3(first), split3(second)
    pieces = [a[p] for p in order] + [b[p] for p in order]
    pad = jnp.zeros((256 - 12 * first.shape[0], first.shape[1]), F32)
    return jnp.concatenate(pieces + [pad], axis=0)


def tile_kernel(
    total, rows_step,
    lf_ref, rf_ref, ld_ref, la_ref, rd_ref, ra_ref, cs_ref, rs_ref,
    tile_ref, row_ref, col_ref,
    left_scr, sketch_scr,
):
    step = pl.program_id(0)
    rows = left_scr.shape[0]

    @pl.when(step == 0)
    def _():
        for r in range(0, rows, 512):
            stacked = stack_parts(la_ref[:, r:r + 512], -ld_ref[:, r:r + 512], LEFT_PARTS)
            left_scr[r:r + 512, :] = stacked.T.astype(BF16)
            sketch_scr[:, r:r + 512] = rs_ref[r:r + 512, :].astype(F32).T.astype(BF16)
        row_ref[...] = jnp.zeros_like(row_ref)

    right = stack_parts(rd_ref[...], ra_ref[...], RIGHT_PARTS).astype(BF16)
    freq = rf_ref[...]
    acc = jnp.zeros((256, right.shape[1]), F32)
    for chunk in range(rows // rows_step):
        sl = pl.ds(chunk * rows_step, rows_step)
        numer = jnp.dot(left_scr[sl, :], right, preferred_element_type=F32)
        gap = total * (lf_ref[sl, :] - freq)
        tile = (numer / gap).astype(BF16)
        tile_ref[sl, :] = tile
        row_ref[sl, :] += jnp.dot(tile, cs_ref[...], preferred_element_type=F32)
        acc += jnp.dot(sketch_scr[:, sl], tile, preferred_element_type=F32)
    col_ref[...] = acc.T


def build(lf, rf, ld, la, rd, ra, cs, rs, total):
    rows, cols = lf.shape[0], rf.shape[0]
    ports, width = ld.shape[0], cs.shape[1]
    tc = 256
    fixed = lambda j: (0, 0)
    return pl.pallas_call(
        functools.partial(tile_kernel, float(total), 256),
        grid=(cols // tc,),
        in_specs=[
            pl.BlockSpec((rows, 1), fixed),
            pl.BlockSpec((1, tc), lambda j: (0, j)),
            pl.BlockSpec((ports, rows), fixed),
            pl.BlockSpec((ports, rows), fixed),
            pl.BlockSpec((ports, tc), lambda j: (0, j)),
            pl.BlockSpec((ports, tc), lambda j: (0, j)),
            pl.BlockSpec((tc, width), lambda j: (j, 0)),
            pl.BlockSpec((rows, width), fixed),
        ],
        out_specs=[
            pl.BlockSpec((rows, tc), lambda j: (0, j)),
            pl.BlockSpec((rows, width), fixed),
            pl.BlockSpec((tc, width), lambda j: (j, 0)),
        ],
        out_shape=[
            jax.ShapeDtypeStruct((rows, cols), BF16),
            jax.ShapeDtypeStruct((rows, width), F32),
            jax.ShapeDtypeStruct((cols, width), F32),
        ],
        scratch_shapes=[pltpu.VMEM((rows, 256), BF16), pltpu.VMEM((width, rows), BF16)],
        compiler_params=pltpu.CompilerParams(
            dimension_semantics=("arbitrary",), vmem_limit_bytes=40 << 20
        ),
        name="tiles",
    )(lf[:, None], rf[None, :], ld, la, rd, ra, cs, rs)


BLOCK = 32


def chol_kernel(shifted, g_ref, out_ref, work):
    width = g_ref.shape[-1]
    row_id = lax.broadcasted_iota(jnp.int32, (width, width), 0)
    col_id = lax.broadcasted_iota(jnp.int32, (width, width), 1)
    eye = (row_id == col_id).astype(F32)
    for m in range(2):
        gram = g_ref[m]
        if shifted:
            trace = jnp.sum(jnp.sum(gram * eye, axis=1, keepdims=True), axis=0, keepdims=True)
            gram = gram + (1e-05 * trace / width) * eye
        work[m, :, 0:width] = gram
        work[m, :, width:] = eye
    brow = lax.broadcasted_iota(jnp.int32, (BLOCK, BLOCK), 0)
    bcol = lax.broadcasted_iota(jnp.int32, (BLOCK, BLOCK), 1)
    small_eye = (brow == bcol).astype(F32)
    for k in range(0, width, BLOCK):
        for m in range(2):
            block = work[m, k:k + BLOCK, k:k + BLOCK]
            pair = jnp.concatenate([block, small_eye], axis=1)
            low = lax.broadcasted_iota(jnp.int32, pair.shape, 0)
            scale = jnp.ones((BLOCK, 1), F32)
            for s in range(BLOCK):
                pivot = pair[s:s + 1, :]
                top = 1.0 / pair[s:s + 1, s:s + 1]
                column = jnp.where(low > s, pair[:, s:s + 1], 0.0)
                pair = pair - column * (pivot * top)
            diag = jnp.sum(pair[:, 0:BLOCK] * small_eye, axis=1, keepdims=True)
            inv = pair[:, BLOCK:] * lax.rsqrt(diag)
            rows = jnp.dot(
                inv, work[m, k:k + BLOCK, :], precision=precise, preferred_element_type=F32
            )
            out_ref[m, k:k + BLOCK, :] = rows[:, width:]
            if k + BLOCK < width:
                lo = k + BLOCK
                work[m, lo:, :] = work[m, lo:, :] - tdot(rows[:, lo:width], rows, precise)


def chol_inverse(grams, shifted):
    width = grams.shape[-1]
    return pl.pallas_call(
        functools.partial(chol_kernel, shifted),
        in_specs=[pl.BlockSpec(memory_space=pltpu.VMEM)],
        out_specs=pl.BlockSpec(memory_space=pltpu.VMEM),
        out_shape=jax.ShapeDtypeStruct((2, width, width), F32),
        scratch_shapes=[pltpu.VMEM((2, width, 2 * width), F32)],
        compiler_params=pltpu.CompilerParams(vmem_limit_bytes=32 << 20),
        name="factor",
    )(grams)


def apply_inverse(basis, inverse):
    return lax.dot_general(
        basis, inverse, (((1,), (1,)), ((), ())), precision=precise, preferred_element_type=F32
    )


def body(lf, rf, ld, la, rd, ra, cs, rs):
    rows, cols = lf.shape[0], rf.shape[0]
    left_n, right_n = lax.axis_size("left"), lax.axis_size("right")
    total_rows, total_cols = rows * left_n, cols * right_n
    tile, row_full, col_full = build(lf, rf, ld, la, rd, ra, cs, rs, total_rows)
    row_full = lax.psum(row_full, "right")
    col_full = lax.psum(col_full, "left")
    for sweep in range(2):
        gram_rows = lax.psum(tdot(row_full, row_full, precise), "left")
        gram_cols = lax.psum(tdot(col_full, col_full, precise), "right")
        inverse = chol_inverse(jnp.stack([gram_rows, gram_cols]), sweep == 0)
        row_full = apply_inverse(row_full, inverse[0])
        col_full = apply_inverse(col_full, inverse[1])
    share = rows // right_n
    row_part = lax.dynamic_slice_in_dim(row_full, lax.axis_index("right") * share, share, 0)
    col_round = col_full.astype(BF16)
    applied = jnp.dot(tile, col_round, preferred_element_type=F32)
    both = jnp.concatenate([applied, applied * lf[:, None]], axis=1)
    reduced = tdot(row_full, both, precise)
    low_rank = jnp.dot(
        lax.dot_general(row_full, ld, (((0,), (1,)), ((), ())), precision=precise),
        jnp.dot(ra, col_round.astype(F32), precision=precise) * (1.0 / total_rows),
        precision=precise,
    )
    width = cs.shape[1]
    reduced = jnp.concatenate([reduced[:, :width], reduced[:, width:] + low_rank], axis=1)
    reduced = lax.psum(reduced, ("left", "right"))
    return (
        row_part * math.sqrt(total_rows),
        col_full * math.sqrt(total_cols),
        reduced[:, :width],
        reduced[:, width:],
    )


def solution(mesh):
    in_specs = (
        P("left"), P("right"), P(None, "left"), P(None, "left"),
        P(None, "right"), P(None, "right"), P("right", None), P("left", None),
    )
    out_specs = (P(("left", "right"), None), P("right", None), P(), P())
    return jax.shard_map(body, mesh=mesh, in_specs=in_specs, out_specs=out_specs, check_vma=False)
```

time: 878 us -> 618 us (0.70)
  other arithmetic: 228 us -> 3.74 us
  matrix products: 190 us -> 81.2 us
  Pallas kernels: 0 us -> 86.1 us
  local copies, waits for them, and re-layouts: 23.8 us -> 12.2 us
    another operation x36 -> x2, other arithmetic: 217 us -> 2.05 us  [body(): inverse = chol_inverse(jnp.stack([gram_rows, gram_cols]), sweep == 0)]
    dot_general x16 -> x13, matrix products: 184 us -> 81.2 us  [the longest x5 41 us: tdot(): lax.dot_general(a, b, (((0,), (0,)), ((), ())), precision=precision, pref...]
    pallas_call x0 -> x3, Pallas kernels: none -> 86.1 us  [the longest x2 59.6 us: chol_inverse(): pl.pallas_call(functools.partial(chol_kernel, shifted), in_specs=[pl.Bloc...]
    another operation x37 -> x0, local copies, waits for them, and re-layouts: 16 us -> none  [the longest x29 15.9 us: apply_factor(): inverse = jax.scipy.linalg.solve_triangular(factor, identity, lower=True)]
where the time goes in v1:
time: 618 us; the launch traced here: 613 us
  waiting for transfers between devices  414 us (67%)
  Pallas kernels  86.1 us (14%)
  matrix products  81.2 us (13%)
  between operations  14.5 us (2%)
  local copies, waits for them, and re-layouts  12.2 us (2%)
    psum x1, waiting for transfers between devices, body(): reduced = lax.psum(reduced, ('left', 'right'))  127 us
    psum x1, waiting for transfers between devices, body(): row_full = lax.psum(row_full, 'right')  89.3 us
    psum x1, waiting for transfers between devices, body(): col_full = lax.psum(col_full, 'left')  83 us
    psum x2, waiting for transfers between devices, body(): gram_cols = lax.psum(tdot(col_full, col_full, precise), 'right')  72.7 us
    pallas_call x2, Pallas kernels, chol_inverse(): pl.pallas_call(functools.partial(chol_kernel, shifted), in_specs=[pl.Bloc...  59.6 us
    psum x1, waiting for transfers between devices, body(): gram_rows = lax.psum(tdot(row_full, row_full, precise), 'left')  42 us
    dot_general x5, matrix products, tdot(): lax.dot_general(a, b, (((0,), (0,)), ((), ())), precision=precision, pref...  41 us
    pallas_call x1, Pallas kernels, build(): pl.pallas_call(functools.partial(tile_kernel, float(total), 256), grid=(c...  26.4 us
  transfers between devices with their start and end apart: 6, of which 6 were waited for; matrix products, arithmetic and copies ran while one was open for 2% of the time, Pallas kernels for 0%

profile of v1, /device:TPU:0, one launch (start us, length us, event | category | flops | bytes accessed | tf_op | source)
XLA Modules:
  0.0 612.8 jit_solution(12991038560973285885)
XLA Ops:
  7.2 1.1 copy.13.lf_ref
  8.3 1.6 copy-done.1
  9.9 1.2 copy-done.2
  11.1 0.9 copy-done.3
  12.1 0.9 copy-done.5
  13.0 0.9 copy-done.7
  13.9 0.9 copy-done.8
  15.5 26.4 %tiles.1 = (bf16[2048,4096]{1,0:T(8,128)(2,1)}, f32[2048,256]{1,0:T(8,128)}, f32[4096,256]{1,0:T(8,128)S(1)}) custom-call(f32[2048,1]{1,0:T(8,128)S(1)} %copy.13.lf_ref, f32[1,4096]{1,0:T(1,128)S(1)} %bitcast.45, f32[16,2048]{1,0:T(8,128)S(1)} %copy-done.5, f32[16,2048]{1,0:T(8,128)S(1)} %copy-done.8, f32[16,4096]{1,0:T(8,128)S(1)} %copy-done.7, ...), custom_call_target="tpu_custom_call" | custom-call | tf_op jit(solution)/shard_map/tiles/pallas_call | solution.py:74
  41.9 2.0 copy-done
  44.0 89.3 %all-reduce.8.cloned.1.call-done = f32[2048,256]{1,0:T(8,128)} async-done(((f32[2048,256]{1,0:T(8,128)}), f32[2048,256]{1,0:T(8,128)}) %all-reduce.8.cloned.1.call-update) | async-done | bytes 2097168 | tf_op jit(solution)/shard_map/psum | solution.py:169
  133.3 6.4 %convolution_bitcast_fusion.3 = f32[1,256,256]{2,1,0:T(8,128)} fusion(f32[2048,256]{1,0:T(8,128)} %all-reduce.8.cloned.1.call-done), kind=kOutput, calls=%fused_computation.9 | convolution fusion | flops 1610612736 | bytes 2359296 | tf_op jit(solution)/shard_map/dot_general | solution.py:19
  140.1 83.0 %all-reduce.18.cloned.1.call-done = (f32[4096,256]{1,0:T(8,128)}, f32[1,256,256]{2,1,0:T(8,128)}) async-done(((f32[4096,256]{1,0:T(8,128)}, f32[1,256,256]{2,1,0:T(8,128)}), (f32[4096,256]{1,0:T(8,128)}, f32[1,256,256]{2,1,0:T(8,128)})) %all-reduce.18.cloned.1.call-update) | async-done | bytes 4456464 | tf_op jit(solution)/shard_map/psum | solution.py:170
  223.0 10.9 %convolution_bitcast_fusion.1 = f32[1,256,256]{2,1,0:T(8,128)} fusion(f32[4096,256]{1,0:T(8,128)} %get-tuple-element.10), kind=kOutput, calls=%fused_computation.7 | convolution fusion | flops 3221225472 | bytes 4456448 | tf_op jit(solution)/shard_map/dot_general | solution.py:19
  234.5 35.1 %all-reduce.10.cloned.1.call-done = f32[1,256,256]{2,1,0:T(8,128)} async-done(((f32[1,256,256]{2,1,0:T(8,128)}), f32[1,256,256]{2,1,0:T(8,128)}) %all-reduce.10.cloned.1.call-update) | async-done | bytes 262160 | tf_op jit(solution)/shard_map/psum | solution.py:173
  269.5 1.0 pad_maximum_fusion.g_ref
  270.5 30.0 %factor.2 = f32[2,256,256]{2,1,0:T(8,128)S(1)} custom-call(f32[2,256,256]{2,1,0:T(8,128)S(1)} %pad_maximum_fusion.g_ref), custom_call_target="tpu_custom_call" | custom-call | tf_op jit(solution)/shard_map/factor/pallas_call | solution.py:147
  300.5 8.0 %fusion.9 = f32[4096,256]{1,0:T(8,128)} fusion(f32[4096,256]{1,0:T(8,128)} %get-tuple-element.10, f32[2,256,256]{2,1,0:T(8,128)S(1)} %factor.2), kind=kOutput, calls=%fused_computation.24 | convolution fusion | flops 3221225472 | bytes 8650752 | tf_op jit(solution)/shard_map/dot_general | solution.py:159
  308.5 1.8 fusion.10
  310.3 4.2 convolution_bitcast_fusion.2
  314.6 10.9 %convolution_bitcast_fusion = f32[1,256,256]{2,1,0:T(8,128)} fusion(f32[4096,256]{1,0:T(8,128)} %fusion.9), kind=kOutput, calls=%fused_computation.6 | convolution fusion | flops 3221225472 | bytes 4456448 | tf_op jit(solution)/shard_map/dot_general | solution.py:19
  326.0 42.0 %all-reduce.12.cloned.1.call-done = f32[1,256,256]{2,1,0:T(8,128)} async-done(((f32[1,256,256]{2,1,0:T(8,128)}), f32[1,256,256]{2,1,0:T(8,128)}) %all-reduce.12.cloned.1.call-update) | async-done | bytes 262160 | tf_op jit(solution)/shard_map/psum | solution.py:172
  367.9 37.6 %all-reduce.14.cloned.1.call-done = f32[1,256,256]{2,1,0:T(8,128)} async-done(((f32[1,256,256]{2,1,0:T(8,128)}), f32[1,256,256]{2,1,0:T(8,128)}) %all-reduce.14.cloned.1.call-update) | async-done | bytes 262160 | tf_op jit(solution)/shard_map/psum | solution.py:173
  405.5 1.1 pad_maximum_fusion.1.g_ref
  406.6 29.7 %factor.3 = f32[2,256,256]{2,1,0:T(8,128)S(1)} custom-call(f32[2,256,256]{2,1,0:T(8,128)S(1)} %pad_maximum_fusion.1.g_ref), custom_call_target="tpu_custom_call" | custom-call | tf_op jit(solution)/shard_map/factor/pallas_call | solution.py:147
  436.3 7.9 %broadcast_multiply_fusion = (f32[4096,256]{1,0:T(8,128)}, bf16[4096,256]{1,0:T(8,128)(2,1)S(1)}) fusion(f32[4096,256]{1,0:T(8,128)} %fusion.9, f32[2,256,256]{2,1,0:T(8,128)S(1)} %factor.3), kind=kOutput, calls=%fused_computation.4 | convolution fusion | flops 3223322624 | bytes 10747904 | tf_op jit(solution)/shard_map/dot_general | solution.py:159
  444.2 3.2 fusion.8
  447.3 2.3 convolution_multiply_fusion
  449.7 13.0 %broadcast_multiply_fusion.1 = (f32[2048,256]{0,1:T(8,128)}, f32[2048,256]{0,1:T(8,128)}) fusion(f32[2048]{0:T(1024)S(1)} %copy-done.15, bf16[2048,4096]{1,0:T(8,128)(2,1)} %get-tuple-element.9, bf16[4096,256]{1,0:T(8,128)(2,1)} %copy-done.12), kind=kOutput, calls=%fused_computation.11 | convolution fusion | flops 4295491584 | bytes 23076864 | tf_op jit(solution)/shard_map/dot_general | solution.py:180
  462.7 3.6 fusion.13
  466.4 8.5 %fusion = f32[256,512]{1,0:T(8,128)S(1)} fusion(f32[2048,256]{1,0:T(8,128)S(1)} %copy-done.10, f32[2048,256]{0,1:T(8,128)S(1)} %copy-done.13, f32[2048,256]{0,1:T(8,128)} %get-tuple-element.17), kind=kOutput, calls=%fused_computation | convolution fusion | flops 3222274048 | bytes 6815744 | tf_op jit(solution)/shard_map/dot_general | solution.py:19
  477.0 126.9 %all-reduce.16.cloned.1.call-done = f32[256,512]{1,0:T(8,128)} async-done(((f32[256,512]{1,0:T(8,128)}), f32[256,512]{1,0:T(8,128)}) %all-reduce.16.cloned.1.call-update) | async-done | bytes 524304 | tf_op jit(solution)/shard_map/psum | solution.py:190
  603.9 1.9 fusion.12
  (41 shorter events, 4.2 us)
Async XLA Ops:
  7.2 126.2 %all-reduce.8.cloned.1.call-start = ((), (), s32[]{:S(2)}) async-start(), calls=%async_computation | async-start | bytes 4194304 | tf_op jit(solution)/shard_map/psum | solution.py:169
  8.3 1.6 copy-start.1
  9.9 1.2 copy-start.2
  11.1 0.9 copy-start.3
  12.0 0.9 copy-start.5
  13.0 0.9 copy-start.7
  13.9 0.9 copy-start.8
  14.8 0.7 copy-start.9
  41.9 2.0 copy-start
  44.0 179.0 %all-reduce.18.cloned.1.call-start = ((), (), s32[]{:S(2)}) async-start(), calls=%async_computation.5 | async-start | bytes 8912896 | tf_op jit(solution)/shard_map/psum | solution.py:170
  139.8 129.7 %all-reduce.10.cloned.1.call-start = ((), (), s32[]{:S(2)}) async-start(), calls=%async_computation.1 | async-start | bytes 524288 | tf_op jit(solution)/shard_map/psum | solution.py:173
  223.0 46.5 %copy-start.14 = (f32[1,256,256]{2,1,0:T(8,128)S(1)}, f32[1,256,256]{2,1,0:T(8,128)}, u32[]{:S(2)}) copy-start(f32[1,256,256]{2,1,0:T(8,128)} %get-tuple-element.11) | copy-start | bytes 786436
  234.0 133.9 %all-reduce.12.cloned.1.call-start = ((), (), s32[]{:S(2)}) async-start(), calls=%async_computation.2 | async-start | bytes 524288 | tf_op jit(solution)/shard_map/psum | solution.py:172
  300.5 8.0 %copy-start.11 = (f32[2048,256]{1,0:T(8,128)S(1)}, f32[2048,256]{1,0:T(8,128)}, u32[]{:S(2)}) copy-start(f32[2048,256]{1,0:T(8,128)} %all-reduce.8.cloned.1.call-done) | copy-start | bytes 6291460
  314.5 91.0 %all-reduce.14.cloned.1.call-start = ((), (), s32[]{:S(2)}) async-start(), calls=%async_computation.3 | async-start | bytes 524288 | tf_op jit(solution)/shard_map/psum | solution.py:173
  325.5 278.4 %all-reduce.16.cloned.1.call-start = ((), (), s32[]{:S(2)}) async-start(), calls=%async_computation.4 | async-start | bytes 1048576 | tf_op jit(solution)/shard_map/psum | solution.py:190
  444.1 3.2 copy-start.12
  444.2 3.2 copy-start.4
  447.3 2.3 copy-start.15
  449.6 13.1 %copy-start.6 = (f32[16,2048]{1,0:T(8,128)S(1)}, f32[16,2048]{1,0:T(8,128)}, u32[]{:S(2)}) copy-start(f32[16,2048]{1,0:T(8,128)} %ld_ref.1) | copy-start | bytes 393220
  449.7 13.1 %copy-start.10 = (f32[2048,256]{1,0:T(8,128)S(1)}, f32[2048,256]{1,0:T(8,128)}, u32[]{:S(2)}) copy-start(f32[2048,256]{1,0:T(8,128)} %fusion.8) | copy-start | bytes 6291460
  462.7 3.6 copy-start.13
Sparse Core Ops, SparseCore 0:
  44.1 89.2 all-reduce.7
  139.9 83.0 all-reduce.17
  234.1 35.3 all-reduce.9
  314.6 53.2 all-reduce.11
  370.8 34.6 all-reduce.13
  476.3 127.5 all-reduce.15

commit v2 on v1

--- a/solution.py
+++ b/solution.py
@@ -155,44 +155,294 @@
     )(grams)
 
 
-def apply_inverse(basis, inverse):
+def apply_inverse(basis, inverse, precision):
     return lax.dot_general(
-        basis, inverse, (((1,), (1,)), ((), ())), precision=precise, preferred_element_type=F32
-    )
+        basis, inverse, (((1,), (1,)), ((), ())), precision=precision, preferred_element_type=F32
+    )
+
+
+def places():
+    me, deep = lax.axis_index("left"), lax.axis_index("right")
+    core = lax.rem(me, 2)
+    return me, deep, core, me // 2
+
+
+def chip_peer(chip, core, offset, chips):
+    return {"left": lax.rem(chip + offset, chips) * 2 + core}
+
+
+def greet(chips, deeps):
+    me, deep, core, chip = places()
+    barrier = pltpu.get_barrier_semaphore()
+    peers = [{"left": chip * 2 + (1 - core)}]
+    peers += [chip_peer(chip, core, o, chips) for o in range(1, chips)]
+    peers += [{"right": lax.rem(deep + o, deeps)} for o in range(1, deeps)]
+    for peer in peers:
+        pl.semaphore_signal(
+            barrier, inc=1, device_id=peer, device_id_type=pl.DeviceIdType.MESH
+        )
+    pl.semaphore_wait(barrier, len(peers))
+
+
+def send(src, dst, sems, slot, peer):
+    copy = pltpu.make_async_remote_copy(
+        src_ref=src,
+        dst_ref=dst,
+        send_sem=sems.at[0, slot],
+        recv_sem=sems.at[1, slot],
+        device_id=peer,
+        device_id_type=pl.DeviceIdType.MESH,
+    )
+    copy.start()
+    return copy
+
+
+def scatter_kernel(
+    chips, deeps, row_ref, col_ref, row_out, col_out,
+    deep_buf, core_buf, half_buf, chip_buf, deep_sem, core_sem, chip_sem,
+):
+    me, deep, core, chip = places()
+    greet(chips, deeps)
+    share, half, piece = row_out.shape[0], core_buf.shape[0], col_out.shape[0]
+    pair = send(
+        col_ref.at[pl.ds((1 - core) * half, half)], core_buf, core_sem, 0,
+        {"left": chip * 2 + (1 - core)},
+    )
+    deep_copies = []
+    for o in range(1, deeps):
+        peer = lax.rem(deep + o, deeps)
+        deep_copies.append(
+            send(
+                row_ref.at[pl.ds(peer * share, share)], deep_buf.at[o - 1], deep_sem, o - 1,
+                {"right": peer},
+            )
+        )
+    pair.wait()
+
+    @pl.loop(0, chips)
+    def _(p):
+        sl = pl.ds(p * piece, piece)
+        half_buf[sl, :] = col_ref[pl.ds(core * half + p * piece, piece), :] + core_buf[sl, :]
+
+    chip_copies = []
+    for o in range(1, chips):
+        peer = lax.rem(chip + o, chips)
+        chip_copies.append(
+            send(
+                half_buf.at[pl.ds(peer * piece, piece)], chip_buf.at[o - 1], chip_sem, o - 1,
+                {"left": peer * 2 + core},
+            )
+        )
+    col_out[...] = half_buf[pl.ds(chip * piece, piece), :]
+    row_out[...] = row_ref[pl.ds(deep * share, share), :]
+    for o in range(1, chips):
+        chip_copies[o - 1].wait()
+        col_out[...] += chip_buf[o - 1]
+    for o in range(1, deeps):
+        deep_copies[o - 1].wait()
+        row_out[...] += deep_buf[o - 1]
+
+
+def vmem_specs(n):
+    return [pl.BlockSpec(memory_space=pltpu.VMEM)] * n
+
+
+def sem_pair(n):
+    return pltpu.SemaphoreType.DMA((2, n))
+
+
+def comm_params(cid):
+    return pltpu.CompilerParams(
+        collective_id=cid, has_side_effects=True, vmem_limit_bytes=40 << 20
+    )
+
+
+def scatter(row_image, col_image):
+    chips, deeps = lax.axis_size("left") // 2, lax.axis_size("right")
+    rows, width = row_image.shape
+    cols = col_image.shape[0]
+    share, half, piece = rows // deeps, cols // 2, cols // 2 // chips
+    return pl.pallas_call(
+        functools.partial(scatter_kernel, chips, deeps),
+        in_specs=vmem_specs(2),
+        out_specs=vmem_specs(2),
+        out_shape=[
+            jax.ShapeDtypeStruct((share, width), F32),
+            jax.ShapeDtypeStruct((piece, width), F32),
+        ],
+        scratch_shapes=[
+            pltpu.VMEM((deeps - 1, share, width), F32),
+            pltpu.VMEM((half, width), F32),
+            pltpu.VMEM((half, width), F32),
+            pltpu.VMEM((chips - 1, piece, width), F32),
+            sem_pair(deeps - 1), sem_pair(1), sem_pair(chips - 1),
+        ],
+        compiler_params=comm_params(1),
+        name="scatter",
+    )(row_image, col_image)
+
+
+def reduce_kernel(
+    chips, deeps, x_ref, out_ref,
+    core_buf, half_buf, chip_buf, deep_buf,
+    core_sem, chip_sem, deep_sem, back_sem, last_sem,
+):
+    me, deep, core, chip = places()
+    greet(chips, deeps)
+    half, piece = core_buf.shape[0], chip_buf.shape[1]
+    sibling = {"left": chip * 2 + (1 - core)}
+    send(x_ref.at[pl.ds((1 - core) * half, half)], core_buf, core_sem, 0, sibling).wait()
+    half_buf[...] = x_ref[pl.ds(core * half, half), :] + core_buf[...]
+    copies = []
+    for o in range(1, chips):
+        peer = lax.rem(chip + o, chips)
+        copies.append(
+            send(
+                half_buf.at[pl.ds(peer * piece, piece)], chip_buf.at[o - 1], chip_sem, o - 1,
+                {"left": peer * 2 + core},
+            )
+        )
+    part = half_buf[pl.ds(chip * piece, piece), :]
+    for o in range(1, chips):
+        copies[o - 1].wait()
+        part = part + chip_buf[o - 1]
+    deep_buf[deep] = part
+    copies = []
+    for o in range(1, deeps):
+        copies.append(
+            send(
+                deep_buf.at[deep], deep_buf.at[deep], deep_sem, o - 1,
+                {"right": lax.rem(deep + o, deeps)},
+            )
+        )
+    for copy in copies:
+        copy.wait()
+    part = deep_buf[0]
+    for d in range(1, deeps):
+        part = part + deep_buf[d]
+    mine = pl.ds(core * half + chip * piece, piece)
+    out_ref[mine, :] = part
+    copies = []
+    for o in range(1, chips):
+        copies.append(
+            send(
+                out_ref.at[mine], out_ref.at[mine], back_sem, o - 1,
+                chip_peer(chip, core, o, chips),
+            )
+        )
+    for copy in copies:
+        copy.wait()
+    own = pl.ds(core * half, half)
+    send(out_ref.at[own], out_ref.at[own], last_sem, 0, sibling).wait()
+
+
+def reduce_all(x, cid):
+    chips, deeps = lax.axis_size("left") // 2, lax.axis_size("right")
+    rows, width = x.shape
+    half, piece = rows // 2, rows // 2 // chips
+    return pl.pallas_call(
+        functools.partial(reduce_kernel, chips, deeps),
+        in_specs=vmem_specs(1),
+        out_specs=vmem_specs(1)[0],
+        out_shape=jax.ShapeDtypeStruct(x.shape, F32),
+        scratch_shapes=[
+            pltpu.VMEM((half, width), F32),
+            pltpu.VMEM((half, width), F32),
+            pltpu.VMEM((chips - 1, piece, width), F32),
+            pltpu.VMEM((deeps, piece, width), F32),
+            sem_pair(1), sem_pair(chips - 1), sem_pair(deeps - 1), sem_pair(chips - 1),
+            sem_pair(1),
+        ],
+        compiler_params=comm_params(cid),
+        name="reduce",
+    )(x)
+
+
+def gather_kernel(
+    chips, deeps, row_ref, col_ref, row_out, col_out, deep_sem, chip_sem, core_sem
+):
+    me, deep, core, chip = places()
+    greet(chips, deeps)
+    share, piece = row_ref.shape[0], col_ref.shape[0]
+    half = piece * chips
+    mine = pl.ds(core * half + chip * piece, piece)
+    deep_copies, chip_copies = [], []
+    for o in range(1, deeps):
+        deep_copies.append(
+            send(
+                row_ref, row_out.at[pl.ds(deep * share, share)], deep_sem, o - 1,
+                {"right": lax.rem(deep + o, deeps)},
+            )
+        )
+    for o in range(1, chips):
+        chip_copies.append(
+            send(
+                col_ref, col_out.at[mine], chip_sem, o - 1, chip_peer(chip, core, o, chips)
+            )
+        )
+    row_out[pl.ds(deep * share, share), :] = row_ref[...]
+    col_out[mine, :] = col_ref[...]
+    for copy in chip_copies:
+        copy.wait()
+    own = pl.ds(core * half, half)
+    pair = send(
+        col_out.at[own], col_out.at[own], core_sem, 0, {"left": chip * 2 + (1 - core)}
+    )
+    for copy in deep_copies:
+        copy.wait()
+    pair.wait()
+
+
+def gather(row_own, col_own):
+    chips, deeps = lax.axis_size("left") // 2, lax.axis_size("right")
+    width = row_own.shape[1]
+    return pl.pallas_call(
+        functools.partial(gather_kernel, chips, deeps),
+        in_specs=vmem_specs(2),
+        out_specs=vmem_specs(2),
+        out_shape=[
+            jax.ShapeDtypeStruct((row_own.shape[0] * deeps, width), F32),
+            jax.ShapeDtypeStruct((col_own.shape[0] * chips * 2, width), F32),
+        ],
+        scratch_shapes=[sem_pair(deeps - 1), sem_pair(chips - 1), sem_pair(1)],
+        compiler_params=comm_params(2),
+        name="gather",
+    )(row_own, col_own)
 
 
 def body(lf, rf, ld, la, rd, ra, cs, rs):
     rows, cols = lf.shape[0], rf.shape[0]
+    width = cs.shape[1]
     left_n, right_n = lax.axis_size("left"), lax.axis_size("right")
     total_rows, total_cols = rows * left_n, cols * right_n
-    tile, row_full, col_full = build(lf, rf, ld, la, rd, ra, cs, rs, total_rows)
-    row_full = lax.psum(row_full, "right")
-    col_full = lax.psum(col_full, "left")
-    for sweep in range(2):
-        gram_rows = lax.psum(tdot(row_full, row_full, precise), "left")
-        gram_cols = lax.psum(tdot(col_full, col_full, precise), "right")
-        inverse = chol_inverse(jnp.stack([gram_rows, gram_cols]), sweep == 0)
-        row_full = apply_inverse(row_full, inverse[0])
-        col_full = apply_inverse(col_full, inverse[1])
-    share = rows // right_n
-    row_part = lax.dynamic_slice_in_dim(row_full, lax.axis_index("right") * share, share, 0)
+    tile, row_image, col_image = build(lf, rf, ld, la, rd, ra, cs, rs, total_rows)
+    row_own, col_own = scatter(row_image, col_image)
+    grams = jnp.concatenate([tdot(row_own, row_own, precise), tdot(col_own, col_own, precise)], 0)
+    inverse = chol_inverse(reduce_all(grams, 3).reshape(2, width, width), True)
+    row_own = apply_inverse(row_own, inverse[0], precise)
+    col_own = apply_inverse(col_own, inverse[1], precise)
+    grams = jnp.concatenate([tdot(row_own, row_own, precise), tdot(col_own, col_own, precise)], 0)
+    inverse = chol_inverse(reduce_all(grams, 3).reshape(2, width, width), False)
+    row_full, col_full = gather(row_own, col_own)
+    row_part = apply_inverse(row_own, inverse[0], precise)
+    col_full = apply_inverse(col_full, inverse[1], lax.Precision.HIGH)
     col_round = col_full.astype(BF16)
     applied = jnp.dot(tile, col_round, preferred_element_type=F32)
     both = jnp.concatenate([applied, applied * lf[:, None]], axis=1)
-    reduced = tdot(row_full, both, precise)
+    reduced = tdot(row_full, both, lax.Precision.HIGH)
     low_rank = jnp.dot(
         lax.dot_general(row_full, ld, (((0,), (1,)), ((), ())), precision=precise),
         jnp.dot(ra, col_round.astype(F32), precision=precise) * (1.0 / total_rows),
         precision=precise,
     )
-    width = cs.shape[1]
     reduced = jnp.concatenate([reduced[:, :width], reduced[:, width:] + low_rank], axis=1)
-    reduced = lax.psum(reduced, ("left", "right"))
+    reduced = jnp.dot(inverse[0], reduced, precision=precise)
+    reduced = reduce_all(jnp.concatenate([reduced[:, :width], reduced[:, width:]], 0), 3)
     return (
         row_part * math.sqrt(total_rows),
         col_full * math.sqrt(total_cols),
-        reduced[:, :width],
-        reduced[:, width:],
+        reduced[:width],
+        reduced[width:],
     )
 
 

time: 618 us -> 300 us (0.49)
  waiting for transfers between devices: 414 us -> 0 us
  Pallas kernels: 86.1 us -> 250 us
  matrix products: 81.2 us -> 37.6 us
  between operations: 14.5 us -> 1.04 us
    psum x6 -> x0, waiting for transfers between devices: 414 us -> none  [the longest x1 127 us: body(): reduced = lax.psum(reduced, ('left', 'right'))]
    pallas_call x0 -> x5, Pallas kernels: none -> 164 us  [the longest x3 83 us: reduce_all(): pl.pallas_call(functools.partial(reduce_kernel, chips, deeps), in_specs=v...]
    dot_general x5, matrix products: 41 us -> 9.92 us  [tdot(): lax.dot_general(a, b, (((0,), (0,)), ((), ())), precision=precision, pref...]
    dot_general x4, matrix products: 20.8 us -> 7.87 us  [apply_inverse(): lax.dot_general(basis, inverse, (((1,), (1,)), ((), ())), precision=preci...]
  transfers between devices with their start and end apart: 6 -> 0, of which waited for: 6 -> 0; matrix products, arithmetic and copies ran while one was open for 2% -> 0% of each run, Pallas kernels for 0% -> 0%
where the time goes in v2:
time: 300 us; the launch traced here: 297 us
  Pallas kernels  250 us (83%)
  matrix products  37.6 us (13%)
  local copies, waits for them, and re-layouts  9.19 us (3%)
    pallas_call x3, Pallas kernels, reduce_all(): pl.pallas_call(functools.partial(reduce_kernel, chips, deeps), in_specs=v...  83 us
    pallas_call x2, Pallas kernels, chol_inverse(): pl.pallas_call(functools.partial(chol_kernel, shifted), in_specs=[pl.Bloc...  59.6 us
    pallas_call x1, Pallas kernels, scatter(): pl.pallas_call(functools.partial(scatter_kernel, chips, deeps), in_specs=...  41.9 us
    pallas_call x1, Pallas kernels, gather(): pl.pallas_call(functools.partial(gather_kernel, chips, deeps), in_specs=v...  39 us
    pallas_call x1, Pallas kernels, build(): pl.pallas_call(functools.partial(tile_kernel, float(total), 256), grid=(c...  25.9 us
    dot_general x1, matrix products, body(): applied = jnp.dot(tile, col_round, preferred_element_type=F32)  12.9 us
    dot_general x5, matrix products, tdot(): lax.dot_general(a, b, (((0,), (0,)), ((), ())), precision=precision, pref...  9.92 us
    dot_general x4, matrix products, apply_inverse(): lax.dot_general(basis, inverse, (((1,), (1,)), ((), ())), precision=preci...  7.87 us

profile of v2, /device:TPU:0, one launch (start us, length us, event | category | flops | bytes accessed | tf_op | source)
XLA Modules:
  0.0 297.5 jit_solution(3307977956080672492)
XLA Ops:
  0.6 1.1 copy.12.lf_ref
  1.7 0.0 copy-start
  1.7 1.6 copy-done
  3.3 1.2 copy-done.1
  4.5 0.9 copy-done.2
  5.5 0.9 copy-done.4
  6.4 0.9 copy-done.6
  7.3 0.9 copy-done.7
  8.2 0.7 copy-done.8
  8.9 25.9 %tiles.1 = (bf16[2048,4096]{1,0:T(8,128)(2,1)}, f32[2048,256]{1,0:T(8,128)S(1)}, f32[4096,256]{1,0:T(8,128)S(1)}) custom-call(f32[2048,1]{1,0:T(8,128)S(1)} %copy.12.lf_ref, f32[1,4096]{1,0:T(1,128)S(1)} %bitcast.42, f32[16,2048]{1,0:T(8,128)S(1)} %copy-done.4, f32[16,2048]{1,0:T(8,128)S(1)} %copy-done.7, f32[16,4096]{1,0:T(8,128)S(1)} %copy-done.6, ...), custom_call_target="tpu_custom_call" | custom-call | tf_op jit(solution)/shard_map/tiles/pallas_call | solution.py:74
  34.8 41.9 %scatter.1 = (f32[512,256]{1,0:T(8,128)S(1)}, f32[512,256]{1,0:T(8,128)S(1)}) custom-call(f32[2048,256]{1,0:T(8,128)S(1)} %get-tuple-element.11.row_ref, f32[4096,256]{1,0:T(8,128)S(1)} %get-tuple-element.12.col_ref), custom_call_target="tpu_custom_call" | custom-call | tf_op jit(solution)/shard_map/scatter/pallas_call | solution.py:265
  76.8 1.0 fusion.18
  77.8 1.0 fusion.19
  78.9 30.3 %reduce.3 = f32[512,256]{1,0:T(8,128)S(1)} custom-call(f32[512,256]{1,0:T(8,128)S(1)} %pad_maximum_fusion.x_ref), custom_call_target="tpu_custom_call" | custom-call | tf_op jit(solution)/shard_map/reduce/pallas_call | solution.py:343
  109.3 30.0 %factor.2 = f32[2,256,256]{2,1,0:T(8,128)S(1)} custom-call(f32[2,256,256]{2,1,0:T(8,128)S(1)} %bitcast.40), custom_call_target="tpu_custom_call" | custom-call | tf_op jit(solution)/shard_map/factor/pallas_call | solution.py:147
  139.2 0.8 fusion.13.row_ref
  140.1 1.0 fusion.20
  141.1 0.6 fusion.12.col_ref
  141.7 1.0 fusion.21
  142.8 21.0 %reduce.4 = f32[512,256]{1,0:T(8,128)S(1)} custom-call(f32[512,256]{1,0:T(8,128)S(1)} %pad_maximum_fusion.1.x_ref), custom_call_target="tpu_custom_call" | custom-call | tf_op jit(solution)/shard_map/reduce/pallas_call | solution.py:343
  163.9 29.7 %factor.3 = f32[2,256,256]{2,1,0:T(8,128)S(1)} custom-call(f32[2,256,256]{2,1,0:T(8,128)S(1)} %bitcast.41), custom_call_target="tpu_custom_call" | custom-call | tf_op jit(solution)/shard_map/factor/pallas_call | solution.py:147
  193.5 39.0 %gather.1 = (f32[2048,256]{1,0:T(8,128)S(1)}, f32[4096,256]{1,0:T(8,128)S(1)}) custom-call(f32[512,256]{1,0:T(8,128)S(1)} %fusion.13.row_ref, f32[512,256]{1,0:T(8,128)S(1)} %fusion.12.col_ref), custom_call_target="tpu_custom_call" | custom-call | tf_op jit(solution)/shard_map/gather/pallas_call | solution.py:399
  232.6 5.0 %broadcast_multiply_fusion = (f32[4096,256]{1,0:T(8,128)}, bf16[4096,256]{1,0:T(8,128)(2,1)}) fusion(f32[4096,256]{1,0:T(8,128)S(1)} %get-tuple-element.15, f32[2,256,256]{2,1,0:T(8,128)S(1)} %factor.3), kind=kOutput, calls=%fused_computation.4 | convolution fusion | flops 1612709888 | bytes 10747904 | tf_op jit(solution)/shard_map/dot_general | solution.py:159
  237.6 12.9 %broadcast_multiply_fusion.1 = (f32[2048,256]{0,1:T(8,128)}, f32[2048,256]{0,1:T(8,128)}) fusion(f32[2048]{0:T(1024)S(1)} %copy-done.10, bf16[2048,4096]{1,0:T(8,128)(2,1)} %get-tuple-element.17, bf16[4096,256]{1,0:T(8,128)(2,1)} %get-tuple-element.23), kind=kOutput, calls=%fused_computation.8 | convolution fusion | flops 4295491584 | bytes 23076864 | tf_op jit(solution)/shard_map/dot_general | solution.py:430
  250.5 5.8 %fusion = f32[256,512]{1,0:T(8,128)S(1)} fusion(f32[2048,256]{1,0:T(8,128)S(1)} %get-tuple-element.16, f32[2048,256]{0,1:T(8,128)} %get-tuple-element.24, f32[2048,256]{0,1:T(8,128)} %get-tuple-element.25), kind=kOutput, calls=%fused_computation | convolution fusion | flops 1611661312 | bytes 6815744 | tf_op jit(solution)/shard_map/dot_general | solution.py:19
  256.4 2.5 convolution_multiply_fusion.1
  258.9 3.4 %fusion.22 = f32[256,16]{1,0:T(8,128)S(1)} fusion(f32[2048,256]{1,0:T(8,128)S(1)} %get-tuple-element.16, f32[16,2048]{1,0:T(8,128)S(1)} %copy-done.5), kind=kOutput, calls=%fused_computation.34 | convolution fusion | flops 100663296 | bytes 2244608 | tf_op jit(solution)/shard_map/dot_general | solution.py:434
  262.3 0.4 convolution_add_fusion
  262.7 0.6 fusion.7
  263.4 31.6 %reduce.5 = f32[512,256]{1,0:T(8,128)S(1)} custom-call(f32[512,256]{1,0:T(8,128)S(1)} %pad_maximum_fusion.2.x_ref), custom_call_target="tpu_custom_call" | custom-call | tf_op jit(solution)/shard_map/reduce/pallas_call | solution.py:343
  295.1 0.8 fusion.16
  295.9 1.4 convolution_multiply_fusion
  (19 shorter events, 0.2 us)
Async XLA Ops:
  1.7 1.6 copy-start
  3.3 1.2 copy-start.1
  4.5 0.9 copy-start.2
  5.5 0.9 copy-start.4
  6.4 0.9 copy-start.6
  7.3 0.9 copy-start.7
  8.2 0.7 copy-start.8
  232.6 5.0 %copy-start.10 = (f32[2048]{0:T(1024)S(1)}, f32[2048]{0:T(1024)}, u32[]{:S(2)}) copy-start(f32[2048]{0:T(1024)} %param.8) | copy-start | bytes 24580
  250.5 5.9 %copy-start.3 = (f32[16,4096]{1,0:T(8,128)S(1)}, f32[16,4096]{1,0:T(8,128)}, u32[]{:S(2)}) copy-start(f32[16,4096]{1,0:T(8,128)} %ra_ref.1) | copy-start | bytes 786436
  250.5 5.9 %copy-start.9 = (bf16[4096,256]{1,0:T(8,128)(2,1)S(1)}, bf16[4096,256]{1,0:T(8,128)(2,1)}, u32[]{:S(2)}) copy-start(bf16[4096,256]{1,0:T(8,128)(2,1)} %get-tuple-element.23) | copy-start | bytes 6291460
  256.4 2.5 copy-start.5

commit v3 on v2

--- a/solution.py
+++ b/solution.py
@@ -39,7 +39,7 @@
     total, rows_step,
     lf_ref, rf_ref, ld_ref, la_ref, rd_ref, ra_ref, cs_ref, rs_ref,
     tile_ref, row_ref, col_ref,
-    left_scr, sketch_scr,
+    left_scr, sketch_scr, freq_scr,
 ):
     step = pl.program_id(0)
     rows = left_scr.shape[0]
@@ -47,6 +47,8 @@
     @pl.when(step == 0)
     def _():
         for r in range(0, rows, 512):
+            wide = jnp.broadcast_to(lf_ref[:, r:r + 512], (128, 512))
+            freq_scr[r:r + 512, :] = wide.T[:, 0:1]
             stacked = stack_parts(la_ref[:, r:r + 512], -ld_ref[:, r:r + 512], LEFT_PARTS)
             left_scr[r:r + 512, :] = stacked.T.astype(BF16)
             sketch_scr[:, r:r + 512] = rs_ref[r:r + 512, :].astype(F32).T.astype(BF16)
@@ -58,7 +60,7 @@
     for chunk in range(rows // rows_step):
         sl = pl.ds(chunk * rows_step, rows_step)
         numer = jnp.dot(left_scr[sl, :], right, preferred_element_type=F32)
-        gap = total * (lf_ref[sl, :] - freq)
+        gap = total * (freq_scr[sl, :] - freq)
         tile = (numer / gap).astype(BF16)
         tile_ref[sl, :] = tile
         row_ref[sl, :] += jnp.dot(tile, cs_ref[...], preferred_element_type=F32)
@@ -75,7 +77,7 @@
         functools.partial(tile_kernel, float(total), 256),
         grid=(cols // tc,),
         in_specs=[
-            pl.BlockSpec((rows, 1), fixed),
+            pl.BlockSpec((1, rows), fixed),
             pl.BlockSpec((1, tc), lambda j: (0, j)),
             pl.BlockSpec((ports, rows), fixed),
             pl.BlockSpec((ports, rows), fixed),
@@ -94,12 +96,16 @@
             jax.ShapeDtypeStruct((rows, width), F32),
             jax.ShapeDtypeStruct((cols, width), F32),
         ],
-        scratch_shapes=[pltpu.VMEM((rows, 256), BF16), pltpu.VMEM((width, rows), BF16)],
+        scratch_shapes=[
+            pltpu.VMEM((rows, 256), BF16),
+            pltpu.VMEM((width, rows), BF16),
+            pltpu.VMEM((rows, 1), F32),
+        ],
         compiler_params=pltpu.CompilerParams(
             dimension_semantics=("arbitrary",), vmem_limit_bytes=40 << 20
         ),
         name="tiles",
-    )(lf[:, None], rf[None, :], ld, la, rd, ra, cs, rs)
+    )(lf[None, :], rf[None, :], ld, la, rd, ra, cs, rs)
 
 
 BLOCK = 32
@@ -120,26 +126,35 @@
     brow = lax.broadcasted_iota(jnp.int32, (BLOCK, BLOCK), 0)
     bcol = lax.broadcasted_iota(jnp.int32, (BLOCK, BLOCK), 1)
     small_eye = (brow == bcol).astype(F32)
+    low = lax.broadcasted_iota(jnp.int32, (BLOCK, 2 * BLOCK), 0)
     for k in range(0, width, BLOCK):
+        pairs = [
+            jnp.concatenate([work[m, k:k + BLOCK, k:k + BLOCK], small_eye], axis=1)
+            for m in range(2)
+        ]
+        for s in range(BLOCK):
+            tops = [1.0 / pair[s:s + 1, s:s + 1] for pair in pairs]
+            columns = [jnp.where(low > s, pair[:, s:s + 1], 0.0) for pair in pairs]
+            pairs = [
+                pair - column * (pair[s:s + 1, :] * top)
+                for pair, column, top in zip(pairs, columns, tops)
+            ]
+        solved = []
         for m in range(2):
-            block = work[m, k:k + BLOCK, k:k + BLOCK]
-            pair = jnp.concatenate([block, small_eye], axis=1)
-            low = lax.broadcasted_iota(jnp.int32, pair.shape, 0)
-            scale = jnp.ones((BLOCK, 1), F32)
-            for s in range(BLOCK):
-                pivot = pair[s:s + 1, :]
-                top = 1.0 / pair[s:s + 1, s:s + 1]
-                column = jnp.where(low > s, pair[:, s:s + 1], 0.0)
-                pair = pair - column * (pivot * top)
-            diag = jnp.sum(pair[:, 0:BLOCK] * small_eye, axis=1, keepdims=True)
-            inv = pair[:, BLOCK:] * lax.rsqrt(diag)
-            rows = jnp.dot(
-                inv, work[m, k:k + BLOCK, :], precision=precise, preferred_element_type=F32
-            )
-            out_ref[m, k:k + BLOCK, :] = rows[:, width:]
-            if k + BLOCK < width:
-                lo = k + BLOCK
-                work[m, lo:, :] = work[m, lo:, :] - tdot(rows[:, lo:width], rows, precise)
+            diag = jnp.sum(pairs[m][:, 0:BLOCK] * small_eye, axis=1, keepdims=True)
+            inv = pairs[m][:, BLOCK:] * lax.rsqrt(diag)
+            solved.append(
+                jnp.dot(
+                    inv, work[m, k:k + BLOCK, :], precision=precise, preferred_element_type=F32
+                )
+            )
+        for m in range(2):
+            out_ref[m, k:k + BLOCK, :] = solved[m][:, width:]
+        lo = k + BLOCK
+        if lo < width:
+            deltas = [tdot(rows[:, lo:width], rows, precise) for rows in solved]
+            for m in range(2):
+                work[m, lo:, :] = work[m, lo:, :] - deltas[m]
 
 
 def chol_inverse(grams, shifted):
@@ -151,6 +166,9 @@
         out_shape=jax.ShapeDtypeStruct((2, width, width), F32),
         scratch_shapes=[pltpu.VMEM((2, width, 2 * width), F32)],
         compiler_params=pltpu.CompilerParams(vmem_limit_bytes=32 << 20),
+        cost_estimate=pl.CostEstimate(
+            flops=20_000_000_000, bytes_accessed=60_000_000, transcendentals=0
+        ),
         name="factor",
     )(grams)
 
@@ -358,56 +376,91 @@
     )(x)
 
 
-def gather_kernel(
-    chips, deeps, row_ref, col_ref, row_out, col_out, deep_sem, chip_sem, core_sem
-):
+def gather_kernel(chips, deeps, col_ref, col_out, chip_sem, core_sem, deep_sem):
     me, deep, core, chip = places()
-    greet(chips, deeps)
-    share, piece = row_ref.shape[0], col_ref.shape[0]
+    barrier = pltpu.get_barrier_semaphore()
+    sibling = {"left": chip * 2 + (1 - core)}
+    for peer in [sibling] + [chip_peer(chip, core, o, chips) for o in range(1, chips)]:
+        pl.semaphore_signal(
+            barrier, inc=1, device_id=peer, device_id_type=pl.DeviceIdType.MESH
+        )
+    pl.semaphore_wait(barrier, chips)
+    piece = col_ref.shape[0]
     half = piece * chips
     mine = pl.ds(core * half + chip * piece, piece)
-    deep_copies, chip_copies = [], []
-    for o in range(1, deeps):
-        deep_copies.append(
-            send(
-                row_ref, row_out.at[pl.ds(deep * share, share)], deep_sem, o - 1,
-                {"right": lax.rem(deep + o, deeps)},
-            )
-        )
-    for o in range(1, chips):
-        chip_copies.append(
+    copies = []
+    for o in range(1, chips):
+        copies.append(
             send(
                 col_ref, col_out.at[mine], chip_sem, o - 1, chip_peer(chip, core, o, chips)
             )
         )
-    row_out[pl.ds(deep * share, share), :] = row_ref[...]
+    pairs = [send(col_ref, col_out.at[mine], core_sem, 0, sibling)]
     col_out[mine, :] = col_ref[...]
-    for copy in chip_copies:
-        copy.wait()
-    own = pl.ds(core * half, half)
-    pair = send(
-        col_out.at[own], col_out.at[own], core_sem, 0, {"left": chip * 2 + (1 - core)}
-    )
-    for copy in deep_copies:
-        copy.wait()
-    pair.wait()
-
-
-def gather(row_own, col_own):
+    for o in range(1, chips):
+        copies[o - 1].wait()
+        came = lax.rem(chip + chips - o, chips)
+        block = pl.ds(core * half + came * piece, piece)
+        pairs.append(send(col_out.at[block], col_out.at[block], core_sem, o, sibling))
+    for pair in pairs:
+        pair.wait()
+
+
+def gather(col_own):
     chips, deeps = lax.axis_size("left") // 2, lax.axis_size("right")
-    width = row_own.shape[1]
+    width = col_own.shape[1]
     return pl.pallas_call(
         functools.partial(gather_kernel, chips, deeps),
-        in_specs=vmem_specs(2),
-        out_specs=vmem_specs(2),
+        in_specs=vmem_specs(1),
+        out_specs=vmem_specs(1)[0],
+        out_shape=jax.ShapeDtypeStruct((col_own.shape[0] * chips * 2, width), F32),
+        scratch_shapes=[sem_pair(chips - 1), sem_pair(chips), sem_pair(1)],
+        compiler_params=comm_params(2),
+        cost_estimate=pl.CostEstimate(
+            flops=20_000_000_000, bytes_accessed=60_000_000, transcendentals=0
+        ),
+        name="gather",
+    )(col_own)
+
+
+def finish_kernel(scale, q_ref, inv_ref, out_ref, round_ref):
+    inv = inv_ref[...]
+    inv_hi = inv.astype(BF16)
+    inv_lo = (inv - inv_hi.astype(F32)).astype(BF16)
+    q = q_ref[...]
+    q_hi = q.astype(BF16)
+    q_lo = (q - q_hi.astype(F32)).astype(BF16)
+    dims = (((1,), (1,)), ((), ()))
+    basis = lax.dot_general(
+        jnp.concatenate([q_hi, q_hi, q_lo], axis=1),
+        jnp.concatenate([inv_hi, inv_lo, inv_hi], axis=1),
+        dims, preferred_element_type=F32,
+    )
+    out_ref[...] = basis * scale
+    round_ref[...] = basis.astype(BF16)
+
+
+def finish(q, inverse, scale):
+    rows, width = q.shape
+    block = 512
+    return pl.pallas_call(
+        functools.partial(finish_kernel, scale),
+        grid=(rows // block,),
+        in_specs=[
+            pl.BlockSpec((block, width), lambda i: (i, 0)),
+            pl.BlockSpec((width, width), lambda i: (0, 0)),
+        ],
+        out_specs=[
+            pl.BlockSpec((block, width), lambda i: (i, 0)),
+            pl.BlockSpec((block, width), lambda i: (i, 0)),
+        ],
         out_shape=[
-            jax.ShapeDtypeStruct((row_own.shape[0] * deeps, width), F32),
-            jax.ShapeDtypeStruct((col_own.shape[0] * chips * 2, width), F32),
-        ],
-        scratch_shapes=[sem_pair(deeps - 1), sem_pair(chips - 1), sem_pair(1)],
-        compiler_params=comm_params(2),
-        name="gather",
-    )(row_own, col_own)
+            jax.ShapeDtypeStruct((rows, width), F32),
+            jax.ShapeDtypeStruct((rows, width), BF16),
+        ],
+        compiler_params=pltpu.CompilerParams(dimension_semantics=("arbitrary",)),
+        name="finish",
+    )(q, inverse)
 
 
 def body(lf, rf, ld, la, rd, ra, cs, rs):
@@ -423,10 +476,10 @@
     col_own = apply_inverse(col_own, inverse[1], precise)
     grams = jnp.concatenate([tdot(row_own, row_own, precise), tdot(col_own, col_own, precise)], 0)
     inverse = chol_inverse(reduce_all(grams, 3).reshape(2, width, width), False)
-    row_full, col_full = gather(row_own, col_own)
+    row_full = lax.all_gather(row_own, "right", axis=0, tiled=True)
+    col_full = gather(col_own)
     row_part = apply_inverse(row_own, inverse[0], precise)
-    col_full = apply_inverse(col_full, inverse[1], lax.Precision.HIGH)
-    col_round = col_full.astype(BF16)
+    col_scaled, col_round = finish(col_full, inverse[1], math.sqrt(total_cols))
     applied = jnp.dot(tile, col_round, preferred_element_type=F32)
     both = jnp.concatenate([applied, applied * lf[:, None]], axis=1)
     reduced = tdot(row_full, both, lax.Precision.HIGH)
@@ -440,7 +493,7 @@
     reduced = reduce_all(jnp.concatenate([reduced[:, :width], reduced[:, width:]], 0), 3)
     return (
         row_part * math.sqrt(total_rows),
-        col_full * math.sqrt(total_cols),
+        col_scaled,
         reduced[:width],
         reduced[width:],
     )

time: 300 us -> 306 us (1.020)
  between operations: 1.04 us -> 14.5 us
  Pallas kernels: 250 us -> 243 us
  matrix products: 37.6 us -> 34.5 us
    pallas_call x1, Pallas kernels: 39 us -> 28.5 us  [gather(): pl.pallas_call(functools.partial(gather_kernel, chips, deeps), in_specs=v...]
    pallas_call x0 -> x1, Pallas kernels: none -> 8.55 us  [finish(): pl.pallas_call(functools.partial(finish_kernel, scale), grid=(rows // blo...]
    dot_general x4 -> x3, matrix products: 7.87 us -> 3.53 us  [apply_inverse(): lax.dot_general(basis, inverse, (((1,), (1,)), ((), ())), precision=preci...]
    pallas_call x2, Pallas kernels: 59.6 us -> 56.4 us  [chol_inverse(): pl.pallas_call(functools.partial(chol_kernel, shifted), in_specs=[pl.Bloc...]
    unnamed x22 -> x30, local copies, waits for them, and re-layouts: 7.26 us -> 9.88 us
  transfers between devices with their start and end apart: 0 -> 1, of which waited for: 0 -> 0; matrix products, arithmetic and copies ran while one was open for 0% -> 7% of each run, Pallas kernels for 0% -> 30%
where the time goes in v3:
time: 306 us; the launch traced here: 303 us
  Pallas kernels  243 us (79%)
  matrix products  34.5 us (11%)
  between operations  14.5 us (5%)
  local copies, waits for them, and re-layouts  11.5 us (4%)
    pallas_call x3, Pallas kernels, reduce_all(): pl.pallas_call(functools.partial(reduce_kernel, chips, deeps), in_specs=v...  81.2 us
    pallas_call x2, Pallas kernels, chol_inverse(): pl.pallas_call(functools.partial(chol_kernel, shifted), in_specs=[pl.Bloc...  56.4 us
    pallas_call x1, Pallas kernels, scatter(): pl.pallas_call(functools.partial(scatter_kernel, chips, deeps), in_specs=...  42 us
    pallas_call x1, Pallas kernels, gather(): pl.pallas_call(functools.partial(gather_kernel, chips, deeps), in_specs=v...  28.5 us
    pallas_call x1, Pallas kernels, build(): pl.pallas_call(functools.partial(tile_kernel, float(total), 256), grid=(c...  26.1 us
    dot_general x5, matrix products, tdot(): lax.dot_general(a, b, (((0,), (0,)), ((), ())), precision=precision, pref...  12.2 us
    dot_general x1, matrix products, body(): applied = jnp.dot(tile, col_round, preferred_element_type=F32)  10.5 us
    unnamed x30, local copies, waits for them, and re-layouts  9.88 us
  transfers between devices with their start and end apart: 1, of which 0 were waited for; matrix products, arithmetic and copies ran while one was open for 7% of the time, Pallas kernels for 30%

profile of v3, /device:TPU:0, one launch (start us, length us, event | category | flops | bytes accessed | tf_op | source)
XLA Modules:
  0.0 303.3 jit_solution(1944133365367136566)
XLA Ops:
  7.2 1.6 copy-done.1
  8.8 1.2 copy-done.2
  10.0 0.9 copy-done.3
  11.0 0.9 copy-done.5
  11.9 0.9 copy-done.7
  12.8 0.9 copy-done.8
  13.7 0.7 copy-done.9
  14.5 0.7 copy-done.10
  15.2 26.1 %tiles.1 = (bf16[2048,4096]{1,0:T(8,128)(2,1)}, f32[2048,256]{1,0:T(8,128)S(1)}, f32[4096,256]{1,0:T(8,128)S(1)}) custom-call(f32[1,2048]{1,0:T(1,128)S(1)} %bitcast.39, f32[1,4096]{1,0:T(1,128)S(1)} %bitcast.38, f32[16,2048]{1,0:T(8,128)S(1)} %copy-done.5, f32[16,2048]{1,0:T(8,128)S(1)} %copy-done.8, f32[16,4096]{1,0:T(8,128)S(1)} %copy-done.7, ...), custom_call_target="tpu_custom_call" | custom-call | tf_op jit(solution)/shard_map/tiles/pallas_call | solution.py:76
  41.3 42.0 %scatter.1 = (f32[512,256]{1,0:T(8,128)S(1)}, f32[512,256]{1,0:T(8,128)S(1)}) custom-call(f32[2048,256]{1,0:T(8,128)S(1)} %get-tuple-element.11.row_ref, f32[4096,256]{1,0:T(8,128)S(1)} %get-tuple-element.12.col_ref), custom_call_target="tpu_custom_call" | custom-call | tf_op jit(solution)/shard_map/scatter/pallas_call | solution.py:283
  83.2 1.0 fusion.14
  84.3 1.0 fusion.15
  85.3 30.3 %reduce.3 = f32[512,256]{1,0:T(8,128)S(1)} custom-call(f32[512,256]{1,0:T(8,128)S(1)} %pad_maximum_fusion.x_ref), custom_call_target="tpu_custom_call" | custom-call | tf_op jit(solution)/shard_map/reduce/pallas_call | solution.py:361
  115.7 28.2 %factor.2 = f32[2,256,256]{2,1,0:T(8,128)S(1)} custom-call(f32[2,256,256]{2,1,0:T(8,128)S(1)} %bitcast.36), custom_call_target="tpu_custom_call" | custom-call | flops 20000000000 | bytes 60000000 | tf_op jit(solution)/shard_map/factor/pallas_call | solution.py:162
  143.9 1.5 fusion.9
  145.4 2.6 fusion.16
  148.1 0.6 fusion.8.col_ref
  148.7 1.0 fusion.17
  149.8 25.4 %reduce.4 = f32[512,256]{1,0:T(8,128)S(1)} custom-call(f32[512,256]{1,0:T(8,128)S(1)} %pad_maximum_fusion.1.x_ref), custom_call_target="tpu_custom_call" | custom-call | tf_op jit(solution)/shard_map/reduce/pallas_call | solution.py:361
  175.2 28.2 %factor.3 = f32[2,256,256]{2,1,0:T(8,128)S(1)} custom-call(f32[2,256,256]{2,1,0:T(8,128)S(1)} %bitcast.37), custom_call_target="tpu_custom_call" | custom-call | flops 20000000000 | bytes 60000000 | tf_op jit(solution)/shard_map/factor/pallas_call | solution.py:162
  203.4 0.7 slice_bitcast_fusion.inv_ref
  204.1 28.5 %gather.1.q_ref = f32[4096,256]{1,0:T(8,128)S(1)} custom-call(f32[512,256]{1,0:T(8,128)S(1)} %fusion.8.col_ref), custom_call_target="tpu_custom_call" | custom-call | flops 20000000000 | bytes 60000000 | tf_op jit(solution)/shard_map/gather/pallas_call | solution.py:412
  232.6 1.9 copy-done
  234.5 8.6 %finish.1 = (f32[4096,256]{1,0:T(8,128)}, bf16[4096,256]{1,0:T(8,128)(2,1)}) custom-call(f32[4096,256]{1,0:T(8,128)} %copy-done, f32[256,256]{1,0:T(8,128)} %slice_bitcast_fusion.inv_ref), custom_call_target="tpu_custom_call" | custom-call | tf_op jit(solution)/shard_map/finish/pallas_call | solution.py:446
  243.1 1.4 convolution_multiply_fusion
  244.5 3.9 %convolution_multiply_fusion.1 = f32[256,16]{1,0:T(8,128)S(1)} fusion(bf16[4096,256]{1,0:T(8,128)(2,1)} %get-tuple-element.17, f32[16,4096]{1,0:T(8,128)S(1)} %copy-done.4), kind=kOutput, calls=%fused_computation.6 | convolution fusion | flops 201330688 | bytes 2375680 | tf_op jit(solution)/shard_map/dot_general | solution.py:488
  248.5 10.5 %broadcast_multiply_fusion = (f32[2048,256]{0,1:T(8,128)}, f32[2048,256]{0,1:T(8,128)}) fusion(f32[2048]{0:T(1024)S(1)} %copy-done.11, bf16[2048,4096]{1,0:T(8,128)(2,1)} %get-tuple-element.16, bf16[4096,256]{1,0:T(8,128)(2,1)S(1)} %copy-done.14), kind=kOutput, calls=%fused_computation.7 | convolution fusion | flops 4295491584 | bytes 23076864 | tf_op jit(solution)/shard_map/dot_general | solution.py:483
  259.0 6.5 %fusion = f32[256,512]{1,0:T(8,128)S(1)} fusion(f32[2048,256]{1,0:T(8,128)} %all-gather.2.cloned.1.call-done, f32[2048,256]{0,1:T(8,128)} %get-tuple-element.22, f32[2048,256]{0,1:T(8,128)} %get-tuple-element.23), kind=kOutput, calls=%fused_computation | convolution fusion | flops 1611661312 | bytes 6815744 | tf_op jit(solution)/shard_map/dot_general | solution.py:19
  265.5 3.4 %fusion.18 = f32[256,16]{1,0:T(8,128)S(1)} fusion(f32[2048,256]{1,0:T(8,128)S(1)} %copy-done.13, f32[16,2048]{1,0:T(8,128)S(1)} %copy-done.6), kind=kOutput, calls=%fused_computation.29 | convolution fusion | flops 100663296 | bytes 2244608 | tf_op jit(solution)/shard_map/dot_general | solution.py:487
  269.3 0.6 fusion.4
  270.0 25.5 %reduce.5 = f32[512,256]{1,0:T(8,128)S(1)} custom-call(f32[512,256]{1,0:T(8,128)S(1)} %pad_maximum_fusion.2.x_ref), custom_call_target="tpu_custom_call" | custom-call | tf_op jit(solution)/shard_map/reduce/pallas_call | solution.py:361
  295.5 0.8 fusion.12
  (30 shorter events, 0.6 us)
Async XLA Ops:
  7.2 251.8 %all-gather.2.cloned.1.call-start = ((), (), s32[]{:S(2)}) async-start(), calls=%async_computation | async-start | bytes 2621440 | tf_op jit(solution)/shard_map/all_gather | solution.py:479
  7.2 1.6 copy-start.1
  8.8 1.2 copy-start.2
  10.0 0.9 copy-start.3
  11.0 0.9 copy-start.5
  11.9 0.9 copy-start.7
  12.8 0.9 copy-start.8
  13.7 0.7 copy-start.9
  14.5 0.7 copy-start.10
  232.6 1.9 copy-start
  234.5 8.6 %copy-start.12 = (f32[512,256]{1,0:T(8,128)S(1)}, f32[512,256]{1,0:T(8,128)}, u32[]{:S(2)}) copy-start(f32[512,256]{1,0:T(8,128)} %fusion.9) | copy-start | bytes 1572868
  234.5 10.0 %copy-start.4 = (f32[16,4096]{1,0:T(8,128)S(1)}, f32[16,4096]{1,0:T(8,128)}, u32[]{:S(2)}) copy-start(f32[16,4096]{1,0:T(8,128)} %ra_ref.1) | copy-start | bytes 786436
  243.1 5.3 %copy-start.11 = (f32[2048]{0:T(1024)S(1)}, f32[2048]{0:T(1024)}, u32[]{:S(2)}) copy-start(f32[2048]{0:T(1024)} %param.8) | copy-start | bytes 24580
  243.1 5.3 %copy-start.14 = (bf16[4096,256]{1,0:T(8,128)(2,1)S(1)}, bf16[4096,256]{1,0:T(8,128)(2,1)}, u32[]{:S(2)}) copy-start(bf16[4096,256]{1,0:T(8,128)(2,1)} %get-tuple-element.17) | copy-start | bytes 6291460
  258.9 6.5 %copy-start.6 = (f32[16,2048]{1,0:T(8,128)S(1)}, f32[16,2048]{1,0:T(8,128)}, u32[]{:S(2)}) copy-start(f32[16,2048]{1,0:T(8,128)} %ld_ref.1) | copy-start | bytes 393220
  258.9 6.5 %copy-start.13 = (f32[2048,256]{1,0:T(8,128)S(1)}, f32[2048,256]{1,0:T(8,128)}, u32[]{:S(2)}) copy-start(f32[2048,256]{1,0:T(8,128)} %all-gather.2.cloned.1.call-done) | copy-start | bytes 6291460
Sparse Core Ops, SparseCore 0:
  145.6 51.3 all-gather.1

commit v4 on v3

--- a/solution.py
+++ b/solution.py
@@ -139,22 +139,26 @@
                 pair - column * (pair[s:s + 1, :] * top)
                 for pair, column, top in zip(pairs, columns, tops)
             ]
+        lo = k + BLOCK
+        start, stop = k // 128 * 128, width + (lo + 127) // 128 * 128
         solved = []
         for m in range(2):
             diag = jnp.sum(pairs[m][:, 0:BLOCK] * small_eye, axis=1, keepdims=True)
             inv = pairs[m][:, BLOCK:] * lax.rsqrt(diag)
             solved.append(
                 jnp.dot(
-                    inv, work[m, k:k + BLOCK, :], precision=precise, preferred_element_type=F32
+                    inv, work[m, k:lo, start:stop], precision=precise,
+                    preferred_element_type=F32,
                 )
             )
         for m in range(2):
-            out_ref[m, k:k + BLOCK, :] = solved[m][:, width:]
-        lo = k + BLOCK
+            out_ref[m, k:lo, 0:stop - width] = solved[m][:, width - start:]
+            if stop < 2 * width:
+                out_ref[m, k:lo, stop - width:] = jnp.zeros((BLOCK, 2 * width - stop), F32)
         if lo < width:
-            deltas = [tdot(rows[:, lo:width], rows, precise) for rows in solved]
+            deltas = [tdot(rows[:, lo - start:width - start], rows, precise) for rows in solved]
             for m in range(2):
-                work[m, lo:, :] = work[m, lo:, :] - deltas[m]
+                work[m, lo:, start:stop] = work[m, lo:, start:stop] - deltas[m]
 
 
 def chol_inverse(grams, shifted):
@@ -166,9 +170,6 @@
         out_shape=jax.ShapeDtypeStruct((2, width, width), F32),
         scratch_shapes=[pltpu.VMEM((2, width, 2 * width), F32)],
         compiler_params=pltpu.CompilerParams(vmem_limit_bytes=32 << 20),
-        cost_estimate=pl.CostEstimate(
-            flops=20_000_000_000, bytes_accessed=60_000_000, transcendentals=0
-        ),
         name="factor",
     )(grams)
 
@@ -376,91 +377,155 @@
     )(x)
 
 
-def gather_kernel(chips, deeps, col_ref, col_out, chip_sem, core_sem, deep_sem):
+def reduce_gather_kernel(
+    chips, deeps, x_ref, row_ref, col_ref, out_ref, row_out, col_out,
+    core_buf, half_buf, chip_buf, deep_buf,
+    core_sem, chip_sem, deep_sem, back_sem, last_sem, row_sem, col_sem, pair_sem,
+):
     me, deep, core, chip = places()
-    barrier = pltpu.get_barrier_semaphore()
+    greet(chips, deeps)
+    half, piece = core_buf.shape[0], chip_buf.shape[1]
+    share, block = row_ref.shape[0], col_ref.shape[0]
     sibling = {"left": chip * 2 + (1 - core)}
-    for peer in [sibling] + [chip_peer(chip, core, o, chips) for o in range(1, chips)]:
-        pl.semaphore_signal(
-            barrier, inc=1, device_id=peer, device_id_type=pl.DeviceIdType.MESH
-        )
-    pl.semaphore_wait(barrier, chips)
-    piece = col_ref.shape[0]
-    half = piece * chips
+    first = send(x_ref.at[pl.ds((1 - core) * half, half)], core_buf, core_sem, 0, sibling)
+    rows_mine = pl.ds(deep * share, share)
+    row_copies = []
+    for o in range(1, deeps):
+        row_copies.append(
+            send(
+                row_ref, row_out.at[rows_mine], row_sem, o - 1,
+                {"right": lax.rem(deep + o, deeps)},
+            )
+        )
+    first.wait()
+    half_buf[...] = x_ref[pl.ds(core * half, half), :] + core_buf[...]
+    copies = []
+    for o in range(1, chips):
+        peer = lax.rem(chip + o, chips)
+        copies.append(
+            send(
+                half_buf.at[pl.ds(peer * piece, piece)], chip_buf.at[o - 1], chip_sem, o - 1,
+                {"left": peer * 2 + core},
+            )
+        )
+    cols_mine = pl.ds((core * chips + chip) * block, block)
+    col_copies = []
+    for o in range(1, chips):
+        col_copies.append(
+            send(
+                col_ref, col_out.at[cols_mine], col_sem, o - 1,
+                chip_peer(chip, core, o, chips),
+            )
+        )
+    row_out[rows_mine, :] = row_ref[...]
+    col_out[cols_mine, :] = col_ref[...]
+    part = half_buf[pl.ds(chip * piece, piece), :]
+    for o in range(1, chips):
+        copies[o - 1].wait()
+        part = part + chip_buf[o - 1]
+    deep_buf[deep] = part
+    copies = []
+    for o in range(1, deeps):
+        copies.append(
+            send(
+                deep_buf.at[deep], deep_buf.at[deep], deep_sem, o - 1,
+                {"right": lax.rem(deep + o, deeps)},
+            )
+        )
+    for copy in copies:
+        copy.wait()
+    part = deep_buf[0]
+    for d in range(1, deeps):
+        part = part + deep_buf[d]
     mine = pl.ds(core * half + chip * piece, piece)
+    out_ref[mine, :] = part
     copies = []
     for o in range(1, chips):
         copies.append(
             send(
-                col_ref, col_out.at[mine], chip_sem, o - 1, chip_peer(chip, core, o, chips)
-            )
-        )
-    pairs = [send(col_ref, col_out.at[mine], core_sem, 0, sibling)]
-    col_out[mine, :] = col_ref[...]
-    for o in range(1, chips):
-        copies[o - 1].wait()
-        came = lax.rem(chip + chips - o, chips)
-        block = pl.ds(core * half + came * piece, piece)
-        pairs.append(send(col_out.at[block], col_out.at[block], core_sem, o, sibling))
-    for pair in pairs:
-        pair.wait()
-
-
-def gather(col_own):
+                out_ref.at[mine], out_ref.at[mine], back_sem, o - 1,
+                chip_peer(chip, core, o, chips),
+            )
+        )
+    for copy in col_copies:
+        copy.wait()
+    own = pl.ds(core * chips * block, chips * block)
+    pair = send(col_out.at[own], col_out.at[own], pair_sem, 0, sibling)
+    for copy in copies:
+        copy.wait()
+    own_half = pl.ds(core * half, half)
+    send(out_ref.at[own_half], out_ref.at[own_half], last_sem, 0, sibling).wait()
+    pair.wait()
+    for copy in row_copies:
+        copy.wait()
+
+
+def reduce_gather(x, row_own, col_own):
     chips, deeps = lax.axis_size("left") // 2, lax.axis_size("right")
-    width = col_own.shape[1]
+    rows, width = x.shape
+    half, piece = rows // 2, rows // 2 // chips
     return pl.pallas_call(
-        functools.partial(gather_kernel, chips, deeps),
-        in_specs=vmem_specs(1),
-        out_specs=vmem_specs(1)[0],
-        out_shape=jax.ShapeDtypeStruct((col_own.shape[0] * chips * 2, width), F32),
-        scratch_shapes=[sem_pair(chips - 1), sem_pair(chips), sem_pair(1)],
+        functools.partial(reduce_gather_kernel, chips, deeps),
+        in_specs=vmem_specs(3),
+        out_specs=vmem_specs(3),
+        out_shape=[
+            jax.ShapeDtypeStruct(x.shape, F32),
+            jax.ShapeDtypeStruct((row_own.shape[0] * deeps, width), F32),
+            jax.ShapeDtypeStruct((col_own.shape[0] * chips * 2, width), F32),
+        ],
+        scratch_shapes=[
+            pltpu.VMEM((half, width), F32),
+            pltpu.VMEM((half, width), F32),
+            pltpu.VMEM((chips - 1, piece, width), F32),
+            pltpu.VMEM((deeps, piece, width), F32),
+            sem_pair(1), sem_pair(chips - 1), sem_pair(deeps - 1), sem_pair(chips - 1),
+            sem_pair(1), sem_pair(deeps - 1), sem_pair(chips - 1), sem_pair(1),
+        ],
         compiler_params=comm_params(2),
-        cost_estimate=pl.CostEstimate(
-            flops=20_000_000_000, bytes_accessed=60_000_000, transcendentals=0
-        ),
-        name="gather",
-    )(col_own)
-
-
-def finish_kernel(scale, q_ref, inv_ref, out_ref, round_ref):
-    inv = inv_ref[...]
-    inv_hi = inv.astype(BF16)
-    inv_lo = (inv - inv_hi.astype(F32)).astype(BF16)
-    q = q_ref[...]
+        name="reduce_gather",
+    )(x, row_own, col_own)
+
+
+def project_kernel(lf_ref, tile_ref, v_ref, q_ref, out_ref):
+    @pl.when(pl.program_id(0) == 0)
+    def _():
+        out_ref[...] = jnp.zeros_like(out_ref)
+
+    applied = jnp.dot(tile_ref[...], v_ref[...], preferred_element_type=F32)
+    freq = jnp.broadcast_to(lf_ref[...], (128, lf_ref.shape[1])).T[:, 0:1]
+    both = jnp.concatenate([applied, applied * freq], axis=1)
+    both_hi = both.astype(BF16)
+    both_lo = (both - both_hi.astype(F32)).astype(BF16)
+    q = q_ref[...].T
     q_hi = q.astype(BF16)
     q_lo = (q - q_hi.astype(F32)).astype(BF16)
-    dims = (((1,), (1,)), ((), ()))
-    basis = lax.dot_general(
+    out_ref[...] += jnp.dot(
         jnp.concatenate([q_hi, q_hi, q_lo], axis=1),
-        jnp.concatenate([inv_hi, inv_lo, inv_hi], axis=1),
-        dims, preferred_element_type=F32,
-    )
-    out_ref[...] = basis * scale
-    round_ref[...] = basis.astype(BF16)
-
-
-def finish(q, inverse, scale):
-    rows, width = q.shape
-    block = 512
+        jnp.concatenate([both_hi, both_lo, both_hi], axis=0),
+        preferred_element_type=F32,
+    )
+
+
+def project(lf, tile, v, q):
+    rows, cols = tile.shape
+    width = v.shape[1]
+    block = 256
     return pl.pallas_call(
-        functools.partial(finish_kernel, scale),
+        project_kernel,
         grid=(rows // block,),
         in_specs=[
+            pl.BlockSpec((1, block), lambda i: (0, i)),
+            pl.BlockSpec((block, cols), lambda i: (i, 0)),
+            pl.BlockSpec((cols, width), lambda i: (0, 0)),
             pl.BlockSpec((block, width), lambda i: (i, 0)),
-            pl.BlockSpec((width, width), lambda i: (0, 0)),
-        ],
-        out_specs=[
-            pl.BlockSpec((block, width), lambda i: (i, 0)),
-            pl.BlockSpec((block, width), lambda i: (i, 0)),
-        ],
-        out_shape=[
-            jax.ShapeDtypeStruct((rows, width), F32),
-            jax.ShapeDtypeStruct((rows, width), BF16),
-        ],
-        compiler_params=pltpu.CompilerParams(dimension_semantics=("arbitrary",)),
-        name="finish",
-    )(q, inverse)
+        ],
+        out_specs=pl.BlockSpec((width, 2 * width), lambda i: (0, 0)),
+        out_shape=jax.ShapeDtypeStruct((width, 2 * width), F32),
+        compiler_params=pltpu.CompilerParams(
+            dimension_semantics=("arbitrary",), vmem_limit_bytes=32 << 20
+        ),
+        name="project",
+    )(lf[None, :], tile, v, q)
 
 
 def body(lf, rf, ld, la, rd, ra, cs, rs):
@@ -475,14 +540,12 @@
     row_own = apply_inverse(row_own, inverse[0], precise)
     col_own = apply_inverse(col_own, inverse[1], precise)
     grams = jnp.concatenate([tdot(row_own, row_own, precise), tdot(col_own, col_own, precise)], 0)
-    inverse = chol_inverse(reduce_all(grams, 3).reshape(2, width, width), False)
-    row_full = lax.all_gather(row_own, "right", axis=0, tiled=True)
-    col_full = gather(col_own)
+    grams, row_full, col_full = reduce_gather(grams, row_own, col_own)
+    inverse = chol_inverse(grams.reshape(2, width, width), False)
     row_part = apply_inverse(row_own, inverse[0], precise)
-    col_scaled, col_round = finish(col_full, inverse[1], math.sqrt(total_cols))
-    applied = jnp.dot(tile, col_round, preferred_element_type=F32)
-    both = jnp.concatenate([applied, applied * lf[:, None]], axis=1)
-    reduced = tdot(row_full, both, lax.Precision.HIGH)
+    col_full = apply_inverse(col_full, inverse[1], lax.Precision.HIGH)
+    col_round = col_full.astype(BF16)
+    reduced = project(lf, tile, col_round, row_full)
     low_rank = jnp.dot(
         lax.dot_general(row_full, ld, (((0,), (1,)), ((), ())), precision=precise),
         jnp.dot(ra, col_round.astype(F32), precision=precise) * (1.0 / total_rows),
@@ -493,7 +556,7 @@
     reduced = reduce_all(jnp.concatenate([reduced[:, :width], reduced[:, width:]], 0), 3)
     return (
         row_part * math.sqrt(total_rows),
-        col_scaled,
+        col_full * math.sqrt(total_cols),
         reduced[:width],
         reduced[width:],
     )

time: 306 us -> 284 us (0.928)
  matrix products: 34.5 us -> 17.9 us
  between operations: 14.5 us -> 1.31 us
  Pallas kernels: 243 us -> 248 us
  local copies, waits for them, and re-layouts: 11.5 us -> 14.6 us
    pallas_call x2, Pallas kernels: 37 us -> 71.9 us  [the longest x1 60.4 us: reduce_gather(): pl.pallas_call(functools.partial(reduce_gather_kernel, chips, deeps), in_...]
    pallas_call x3 -> x2, Pallas kernels: 81.2 us -> 51.8 us  [reduce_all(): pl.pallas_call(functools.partial(reduce_kernel, chips, deeps), in_specs=v...]
    dot_general x1 -> x0, matrix products: 10.5 us -> none  [body(): applied = jnp.dot(tile, col_round, preferred_element_type=F32)]
    dot_general x5 -> x4, matrix products: 12.2 us -> 4.12 us  [tdot(): lax.dot_general(a, b, (((0,), (0,)), ((), ())), precision=precision, pref...]
    unnamed x30 -> x24, local copies, waits for them, and re-layouts: 9.88 us -> 13.7 us
    dot_general x3 -> x4, matrix products: 3.53 us -> 7.03 us  [apply_inverse(): lax.dot_general(basis, inverse, (((1,), (1,)), ((), ())), precision=preci...]
  transfers between devices with their start and end apart: 1 -> 0, of which waited for: 0 -> 0; matrix products, arithmetic and copies ran while one was open for 7% -> 0% of each run, Pallas kernels for 30% -> 0%
where the time goes in v4:
time: 284 us; the launch traced here: 282 us
  Pallas kernels  248 us (87%)
  matrix products  17.9 us (6%)
  local copies, waits for them, and re-layouts  14.6 us (5%)
    pallas_call x1, Pallas kernels, reduce_gather(): pl.pallas_call(functools.partial(reduce_gather_kernel, chips, deeps), in_...  60.4 us
    pallas_call x2, Pallas kernels, chol_inverse(): pl.pallas_call(functools.partial(chol_kernel, shifted), in_specs=[pl.Bloc...  55.5 us
    pallas_call x2, Pallas kernels, reduce_all(): pl.pallas_call(functools.partial(reduce_kernel, chips, deeps), in_specs=v...  51.8 us
    pallas_call x1, Pallas kernels, scatter(): pl.pallas_call(functools.partial(scatter_kernel, chips, deeps), in_specs=...  42 us
    pallas_call x1, Pallas kernels, build(): pl.pallas_call(functools.partial(tile_kernel, float(total), 256), grid=(c...  26.5 us
    unnamed x24, local copies, waits for them, and re-layouts  13.7 us
    pallas_call x1, Pallas kernels, project(): pl.pallas_call(project_kernel, grid=(rows // block,), in_specs=[pl.BlockS...  11.5 us
    dot_general x4, matrix products, apply_inverse(): lax.dot_general(basis, inverse, (((1,), (1,)), ((), ())), precision=preci...  7.03 us

profile of v4, /device:TPU:0, one launch (start us, length us, event | category | flops | bytes accessed | tf_op | source)
XLA Modules:
  0.0 281.5 jit_solution(1371826618064043057)
XLA Ops:
  0.6 1.6 copy-done.1
  2.2 1.2 copy-done.2
  3.5 0.9 copy-done.3
  4.4 0.9 copy-done.5
  5.3 0.9 copy-done.7
  6.3 0.9 copy-done.8
  7.2 0.7 copy-done.9
  7.9 0.7 copy-done.11
  8.6 26.5 %tiles.1 = (bf16[2048,4096]{1,0:T(8,128)(2,1)}, f32[2048,256]{1,0:T(8,128)S(1)}, f32[4096,256]{1,0:T(8,128)S(1)}) custom-call(f32[1,2048]{1,0:T(1,128)S(1)} %bitcast.39, f32[1,4096]{1,0:T(1,128)S(1)} %bitcast.41, f32[16,2048]{1,0:T(8,128)S(1)} %copy-done.5, f32[16,2048]{1,0:T(8,128)S(1)} %copy-done.8, f32[16,4096]{1,0:T(8,128)S(1)} %copy-done.7, ...), custom_call_target="tpu_custom_call" | custom-call | tf_op jit(solution)/shard_map/tiles/pallas_call | solution.py:76
  35.1 42.0 %scatter.1 = (f32[512,256]{1,0:T(8,128)S(1)}, f32[512,256]{1,0:T(8,128)S(1)}) custom-call(f32[2048,256]{1,0:T(8,128)S(1)} %get-tuple-element.12.row_ref, f32[4096,256]{1,0:T(8,128)S(1)} %get-tuple-element.13.col_ref), custom_call_target="tpu_custom_call" | custom-call | tf_op jit(solution)/shard_map/scatter/pallas_call | solution.py:284
  77.0 1.0 fusion.11
  78.1 1.0 fusion.12
  79.1 30.3 %reduce.2 = f32[512,256]{1,0:T(8,128)S(1)} custom-call(f32[512,256]{1,0:T(8,128)S(1)} %pad_maximum_fusion.x_ref), custom_call_target="tpu_custom_call" | custom-call | tf_op jit(solution)/shard_map/reduce/pallas_call | solution.py:362
  109.5 27.8 %factor.2 = f32[2,256,256]{2,1,0:T(8,128)S(1)} custom-call(f32[2,256,256]{2,1,0:T(8,128)S(1)} %bitcast.37), custom_call_target="tpu_custom_call" | custom-call | tf_op jit(solution)/shard_map/factor/pallas_call | solution.py:166
  137.3 0.8 fusion.6.row_ref
  138.2 1.1 fusion.13
  139.2 0.6 fusion.5.col_ref
  139.9 1.0 fusion.14
  140.9 60.4 %reduce_gather.1 = (f32[512,256]{1,0:T(8,128)S(1)}, f32[2048,256]{1,0:T(8,128)S(1)}, f32[4096,256]{1,0:T(8,128)S(1)}) custom-call(f32[512,256]{1,0:T(8,128)S(1)} %pad_maximum_fusion.1.x_ref, f32[512,256]{1,0:T(8,128)S(1)} %fusion.6.row_ref, f32[512,256]{1,0:T(8,128)S(1)} %fusion.5.col_ref), custom_call_target="tpu_custom_call" | custom-call | tf_op jit(solution)/shard_map/reduce_gather/pallas_call | solution.py:467
  201.4 27.7 %factor.3 = f32[2,256,256]{2,1,0:T(8,128)S(1)} custom-call(f32[2,256,256]{2,1,0:T(8,128)S(1)} %bitcast.38), custom_call_target="tpu_custom_call" | custom-call | tf_op jit(solution)/shard_map/factor/pallas_call | solution.py:166
  229.1 0.0 copy-start.10
  229.1 4.1 %fusion.8 = (bf16[4096,256]{1,0:T(8,128)(2,1)S(1)}, f32[4096,256]{1,0:T(8,128)}) fusion(f32[4096,256]{1,0:T(8,128)S(1)} %get-tuple-element.17, f32[2,256,256]{2,1,0:T(8,128)S(1)} %factor.3), kind=kOutput, calls=%fused_computation.19 | convolution fusion | flops 1612709888 | bytes 10747904 | tf_op jit(solution)/shard_map/dot_general | solution.py:178
  233.2 5.8 %copy-done = bf16[2048,4096]{1,0:T(8,128)(2,1)S(1)} copy-done((bf16[2048,4096]{1,0:T(8,128)(2,1)S(1)}, bf16[2048,4096]{1,0:T(8,128)(2,1)}, u32[]{:S(2)}) %copy-start) | copy-done | bytes 16777240
  239.0 11.5 %project.1 = f32[256,512]{1,0:T(8,128)S(1)} custom-call(f32[1,2048]{1,0:T(1,128)S(1)} %bitcast.40, bf16[2048,4096]{1,0:T(8,128)(2,1)S(1)} %copy-done, bf16[4096,256]{1,0:T(8,128)(2,1)S(1)} %get-tuple-element.20.v_ref, f32[2048,256]{1,0:T(8,128)S(1)} %get-tuple-element.19.q_ref), custom_call_target="tpu_custom_call" | custom-call | tf_op jit(solution)/shard_map/project/pallas_call | solution.py:513
  250.5 0.0 copy-start.6
  250.5 2.3 convolution_multiply_fusion.1
  252.8 3.4 %fusion.15 = f32[256,16]{1,0:T(8,128)S(1)} fusion(f32[2048,256]{1,0:T(8,128)S(1)} %get-tuple-element.19.q_ref, f32[16,2048]{1,0:T(8,128)S(1)} %copy-done.6), kind=kOutput, calls=%fused_computation.26 | convolution fusion | flops 100663296 | bytes 2244608 | tf_op jit(solution)/shard_map/dot_general | solution.py:550
  256.3 0.4 convolution_add_fusion
  256.7 0.6 fusion
  257.4 21.4 %reduce.3 = f32[512,256]{1,0:T(8,128)S(1)} custom-call(f32[512,256]{1,0:T(8,128)S(1)} %pad_maximum_fusion.2.x_ref), custom_call_target="tpu_custom_call" | custom-call | tf_op jit(solution)/shard_map/reduce/pallas_call | solution.py:362
  278.8 0.8 fusion.9
  279.6 1.4 convolution_multiply_fusion
  (18 shorter events, 0.2 us)
Async XLA Ops:
  0.6 1.6 copy-start.1
  2.2 1.2 copy-start.2
  3.5 0.9 copy-start.3
  4.4 0.9 copy-start.5
  5.3 0.9 copy-start.7
  6.3 0.9 copy-start.8
  7.2 0.7 copy-start.9
  7.9 0.7 copy-start.11
  229.1 4.2 %copy-start.10 = (f32[2048]{0:T(1024)S(1)}, f32[2048]{0:T(1024)}, u32[]{:S(2)}) copy-start(f32[2048]{0:T(1024)} %param.8) | copy-start | bytes 24580
  233.2 5.8 %copy-start = (bf16[2048,4096]{1,0:T(8,128)(2,1)S(1)}, bf16[2048,4096]{1,0:T(8,128)(2,1)}, u32[]{:S(2)}) copy-start(bf16[2048,4096]{1,0:T(8,128)(2,1)} %get-tuple-element.18.tile_ref) | copy-start | bytes 50331652
  239.0 11.5 %copy-start.4 = (f32[16,4096]{1,0:T(8,128)S(1)}, f32[16,4096]{1,0:T(8,128)}, u32[]{:S(2)}) copy-start(f32[16,4096]{1,0:T(8,128)} %ra_ref.1) | copy-start | bytes 786436
  250.5 2.3 copy-start.6
